TPU v7x, 32 devices: a whole 2x2x4 slice. The times are simulated.
32 devices in a mesh: batch: 4 (over x, core), tiles: 8 (over z, y).
Axes of the slice: x: 2, y: 2, z: 4, core: 2. Of those that a mesh axis runs over, the one named last changes fastest.
Arguments:
- hidden: bfloat16 [4, 4096, 3072], P('batch', 'tiles'), may hold values from -6 to 6
- frozen_queries: bfloat16 [4, 4096, 1536], P('batch', 'tiles'), may hold values from -108 to 108
- frozen_keys: bfloat16 [4, 4096, 1536], P('batch', 'tiles'), may hold values from -6.09 to 6.09
- frozen_values: bfloat16 [4, 4096, 1536], P('batch', 'tiles'), may hold values from -6 to 6
- reward_output_gradient: bfloat16 [4, 4096, 1536], P('batch', 'tiles'), may hold values from -6 to 6
- truncation_step: int32 [4], P('batch'), may hold values from 0 to 49
- modulation: float32 [50, 2, 3072], replicated, may hold values from -3 to 3
- adapter_down_weight: bfloat16 [3, 3072, 32], replicated, may hold values from -0.109375 to 0.109375
- adapter_up_weight: bfloat16 [3, 32, 1536], replicated, may hold values from -1 to 1
- window: int32 [32, 27], P('tiles'), may hold values from 0 to 1, as said below
Outputs:
- attended: bfloat16 [4, 4096, 1536], P('batch', 'tiles')
- grad_down: float32 [3, 3072, 32], replicated
- grad_up: float32 [3, 32, 1536], replicated
Inputs may be any that keep to these rules, and one draw needn't show every extreme that they name: `window`: entry 13, the tile itself, is 1 for every tile.
All inputs are finite; a program needn't handle non-finite values.
Results may differ from a plain program's by a relative error of at most 0.012.
The roundings to bfloat16 on the way count: a program that leaves them out, or rounds other values in their place, can miss the bound.
Values may be sent and summed in bfloat16 or wider, within the bound.
A program may use at most 192 MiB of HBM per device.

v0:
```python
import functools
import math

import jax
import jax.numpy as jnp
from jax import lax
from jax.experimental import pallas as pl
from jax.experimental.pallas import tpu as pltpu
from jax.sharding import PartitionSpec as P

HEAD = 128
TILE = 128
GF = 2
GR = 2
LANES = 128


def dot_nt(a, b):
    return lax.dot_general(
        a, b, (((1,), (1,)), ((), ())), preferred_element_type=jnp.float32
    )


def dot_tn(a, b):
    return lax.dot_general(
        a, b, (((0,), (0,)), ((), ())), preferred_element_type=jnp.float32
    )


def dot_nn(a, b):
    return jnp.dot(a, b, preferred_element_type=jnp.float32)


def project_kernel(step_ref, hidden_ref, mod_ref, down_ref, up_ref, fq_ref, fk_ref, fv_ref,
                   x_ref, low_ref, q_ref, kv_ref):
    x = hidden_ref[0].astype(jnp.float32)
    width = x.shape[1]
    mean = jnp.sum(x, axis=1, keepdims=True) * (1.0 / width)
    centred = x - mean
    variance = jnp.sum(centred * centred, axis=1, keepdims=True) * (1.0 / width)
    normed = centred * lax.rsqrt(variance + 1e-06)
    modulated = normed * (1.0 + mod_ref[0, 1:2, :]) + mod_ref[0, 0:1, :]
    x_low = modulated.astype(jnp.bfloat16)
    x_ref[...] = x_low
    rank = up_ref.shape[1]
    low_ref[...] = jnp.zeros_like(low_ref)
    sums = []
    for j, frozen_ref in enumerate((fq_ref, fk_ref, fv_ref)):
        low = dot_nt(x_low, down_ref[j]).astype(jnp.bfloat16)
        low_ref[:, j * rank:(j + 1) * rank] = low
        total = frozen_ref[0].astype(jnp.float32) + dot_nn(low, up_ref[j])
        sums.append(total.astype(jnp.bfloat16))
    q_ref[...], keys, values = sums
    for h in range(keys.shape[1] // HEAD):
        kv_ref[h, :, 0:HEAD] = keys[:, h * HEAD:(h + 1) * HEAD]
        kv_ref[h, :, HEAD:] = values[:, h * HEAD:(h + 1) * HEAD]


def project(step, hidden, modulation, down, up, fq, fk, fv):
    _, rows, width = hidden.shape
    across = fq.shape[2]
    block = TILE
    heads = across // HEAD
    row3 = lambda i, s: (0, i, 0)
    row2 = lambda i, s: (i, 0)
    return pl.pallas_call(
        project_kernel,
        out_shape=[
            jax.ShapeDtypeStruct((rows, width), jnp.bfloat16),
            jax.ShapeDtypeStruct((rows, LANES), jnp.bfloat16),
            jax.ShapeDtypeStruct((rows, across), jnp.bfloat16),
            jax.ShapeDtypeStruct((heads, rows, 2 * HEAD), jnp.bfloat16),
        ],
        grid_spec=pltpu.PrefetchScalarGridSpec(
            num_scalar_prefetch=1,
            grid=(rows // block,),
            in_specs=[
                pl.BlockSpec((1, block, width), row3),
                pl.BlockSpec((1, 2, width), lambda i, s: (s[0], 0, 0)),
                pl.BlockSpec(down.shape, lambda i, s: (0, 0, 0)),
                pl.BlockSpec(up.shape, lambda i, s: (0, 0, 0)),
                pl.BlockSpec((1, block, across), row3),
                pl.BlockSpec((1, block, across), row3),
                pl.BlockSpec((1, block, across), row3),
            ],
            out_specs=[
                pl.BlockSpec((block, width), row2),
                pl.BlockSpec((block, LANES), row2),
                pl.BlockSpec((block, across), row2),
                pl.BlockSpec((heads, block, 2 * HEAD), lambda i, s: (0, i, 0)),
            ],
        ),
        name="project",
    )(step, hidden, modulation, down, up, fq, fk, fv)


def attend_kernel(rank, count, bias_ref, low_ref, up_ref, q_hbm, g_hbm, kv_hbm,
                  att_ref, rq_ref, own_ref, gup_ref,
                  q_ref, g_ref, kv_ref, kv_swap, kv_relay, low_swap, low_relay, kl, vl, probs_s, grad_s, rkv,
                  r_out, r_in, swap_send, swap_recv, relay_send, relay_recv,
                  low_send, low_recv, r_send, r_recv, load):
    heads, rows = kv_ref.shape[0], q_ref.shape[0]
    index = lax.axis_index("tiles")
    odd = lax.rem(index, 2)
    partner = index + 1 - 2 * odd
    target = lax.rem(index + 2 - 4 * odd + count, count)
    source = lax.rem(index - 2 + 4 * odd + count, count)
    other = lax.rem(index - 1 + 2 * odd + count, count)
    barrier = pltpu.get_barrier_semaphore()
    for peer in (partner, target, source, other):
        pl.semaphore_signal(barrier, inc=1, device_id={"tiles": peer},
                            device_id_type=pl.DeviceIdType.MESH)
    pl.semaphore_wait(barrier, 4)

    def remote(src, dst, send, recv, peer):
        return pltpu.make_async_remote_copy(
            src_ref=src, dst_ref=dst, send_sem=send, recv_sem=recv,
            device_id={"tiles": peer}, device_id_type=pl.DeviceIdType.MESH,
        )

    def swap(h):
        return remote(kv_hbm.at[h], kv_swap.at[h], swap_send.at[h], swap_recv.at[h], partner)

    def relay(h):
        return remote(kv_swap.at[h], kv_relay.at[h], relay_send.at[h], relay_recv.at[h], target)

    def each(step):
        lax.fori_loop(0, heads, lambda h, c: (step(h), c)[1], 0)

    low_first = remote(low_ref, low_swap, low_send.at[0], low_recv.at[0], partner)
    low_next = remote(low_swap, low_relay, low_send.at[1], low_recv.at[1], target)
    low_first.start()
    each(lambda h: swap(h).start())
    loads = [
        pltpu.make_async_copy(src, dst, load.at[i])
        for i, (src, dst) in enumerate(((q_hbm, q_ref), (g_hbm, g_ref), (kv_hbm, kv_ref)))
    ]
    for copy in loads:
        copy.start()
    rq_ref[...] = jnp.zeros_like(rq_ref)
    rkv[...] = jnp.zeros_like(rkv)
    for copy in loads:
        copy.wait()
    low_first.wait_recv()
    low_next.start()
    swap(0).wait_recv()
    relay(0).start()
    low_next.wait_recv()
    for s, low in enumerate((low_ref, low_swap, low_relay)):
        kl[s * rows:(s + 1) * rows, HEAD:] = low[...]
        vl[s * rows:(s + 1) * rows, HEAD:] = low[...]
    scale_root = 1.0 / math.sqrt(HEAD)
    scale_two = scale_root * math.log2(math.e)

    def one_head(h, carry):
        @pl.when(h + 1 < heads)
        def _():
            swap(h + 1).wait_recv()
            relay(h + 1).start()

        relay(h).wait_recv()
        for s, part in enumerate((kv_ref, kv_swap, kv_relay)):
            kl[s * rows:(s + 1) * rows, 0:HEAD] = part[h, :, 0:HEAD]
            vl[s * rows:(s + 1) * rows, 0:HEAD] = part[h, :, HEAD:]
        lanes = pl.ds(pl.multiple_of(h * HEAD, HEAD), HEAD)
        for t in range(rows // TILE):
            span = slice(t * TILE, (t + 1) * TILE)
            scores = dot_nt(q_ref[span, lanes], kl[:, 0:HEAD]) * scale_two + bias_ref[t:t + 1, :]
            top = jnp.max(scores, axis=1, keepdims=True)
            weights = jnp.exp2(scores - top)
            inverse = 1.0 / jnp.sum(weights, axis=1, keepdims=True)
            probs = weights * inverse
            prob_grad = dot_nt(g_ref[0, span, lanes], vl[:, 0:HEAD])
            centre = jnp.sum(probs * prob_grad, axis=1, keepdims=True)
            probs_s[span, :] = probs.astype(jnp.bfloat16)
            grad_s[span, :] = (probs * (prob_grad - centre) * scale_root).astype(jnp.bfloat16)

        q_all = q_ref[:, lanes]
        g_all = g_ref[0, :, lanes]
        q_up = dot_nt(up_ref[1, :, lanes], q_all).astype(jnp.bfloat16)
        g_up = dot_nt(up_ref[2, :, lanes], g_all).astype(jnp.bfloat16)
        rkv[0:rank, :] += dot_nn(q_up, grad_s[...])
        rkv[rank:2 * rank, :] += dot_nn(g_up, probs_s[...])
        att = dot_nn(probs_s[...], vl[...])
        att_ref[0, :, lanes] = att[:, 0:HEAD].astype(jnp.bfloat16)
        low_v = att[:, HEAD:].astype(jnp.bfloat16)
        dq = dot_nn(grad_s[...], kl[...])
        dq_low = dq[:, 0:HEAD].astype(jnp.bfloat16)
        low_k = dq[:, HEAD:].astype(jnp.bfloat16)
        rq_ref[...] += dot_nt(up_ref[0, :, lanes], dq_low)
        gup_ref[0:rank, lanes] = dot_tn(low_ref[...], dq_low)[0:rank, :]
        gup_ref[rank:2 * rank, lanes] = dot_tn(low_k, q_all)[rank:2 * rank, :]
        gup_ref[2 * rank:3 * rank, lanes] = dot_tn(low_v, g_all)[2 * rank:3 * rank, :]
        return carry

    lax.fori_loop(0, heads, one_head, 0)
    returns = []
    for s, peer in enumerate((partner, other)):
        r_out[s] = rkv[:, (s + 1) * rows:(s + 2) * rows]
        returns.append(remote(r_out.at[s], r_in.at[s], r_send.at[s], r_recv.at[s], peer))
        returns[-1].start()
    low_first.wait_send()
    low_next.wait_send()
    each(lambda h: swap(h).wait_send())
    each(lambda h: relay(h).wait_send())
    for copy in returns:
        copy.wait()
    own_ref[...] = rkv[:, 0:rows] + r_in[0] + r_in[1]


def attend(count, bias, q, g, kv, low, up):
    rows, across = q.shape
    heads = across // HEAD
    rank = up.shape[1]
    dma = pltpu.SemaphoreType.DMA
    vmem = pl.BlockSpec(memory_space=pltpu.VMEM)
    bf16, f32 = jnp.bfloat16, jnp.float32
    return pl.pallas_call(
        functools.partial(attend_kernel, rank, count),
        out_shape=[
            jax.ShapeDtypeStruct((1, rows, across), bf16),
            jax.ShapeDtypeStruct((rank, rows), f32),
            jax.ShapeDtypeStruct((2 * rank, rows), f32),
            jax.ShapeDtypeStruct((3 * rank, across), f32),
        ],
        in_specs=[vmem] * 3 + [pl.BlockSpec(memory_space=pl.ANY)] * 3,
        out_specs=[vmem] * 4,
        scratch_shapes=[
            pltpu.VMEM(q.shape, bf16), pltpu.VMEM(g.shape, bf16),
            pltpu.VMEM(kv.shape, bf16), pltpu.VMEM(kv.shape, bf16), pltpu.VMEM(kv.shape, bf16),
            pltpu.VMEM(low.shape, bf16), pltpu.VMEM(low.shape, bf16),
            pltpu.VMEM((3 * rows, 2 * HEAD), bf16),
            pltpu.VMEM((3 * rows, 2 * HEAD), bf16),
            pltpu.VMEM((rows, 3 * rows), bf16),
            pltpu.VMEM((rows, 3 * rows), bf16),
            pltpu.VMEM((2 * rank, 3 * rows), f32),
            pltpu.VMEM((2, 2 * rank, rows), f32),
            pltpu.VMEM((2, 2 * rank, rows), f32),
            dma((heads,)), dma((heads,)), dma((heads,)), dma((heads,)),
            dma((2,)), dma((2,)), dma((2,)), dma((2,)), dma((3,)),
        ],
        compiler_params=pltpu.CompilerParams(
            collective_id=1, has_side_effects=True, vmem_limit_bytes=56 << 20
        ),
        name="attend",
    )(bias, low, up, q, g, kv)


def reduce_kernel(nb, nt, terms_ref, out_ref, first, partial, second, final,
                  send1, recv1, send2, recv2, send3, recv3, send4, recv4):
    mine_b = lax.axis_index("batch")
    mine_t = lax.axis_index("tiles")
    barrier = pltpu.get_barrier_semaphore()
    for d in range(1, nb):
        pl.semaphore_signal(barrier, inc=1, device_id={"batch": lax.rem(mine_b + d, nb)},
                            device_id_type=pl.DeviceIdType.MESH)
    for d in range(1, nt):
        pl.semaphore_signal(barrier, inc=1, device_id={"tiles": lax.rem(mine_t + d, nt)},
                            device_id_type=pl.DeviceIdType.MESH)
    pl.semaphore_wait(barrier, nb + nt - 2)

    def launch(source, target, send, recv, axis, peer):
        copy = pltpu.make_async_remote_copy(
            src_ref=source, dst_ref=target, send_sem=send, recv_sem=recv,
            device_id={axis: peer}, device_id_type=pl.DeviceIdType.MESH,
        )
        copy.start()
        return copy

    peers_b = [lax.rem(mine_b + d, nb) for d in range(1, nb)]
    peers_t = [lax.rem(mine_t + 1 + e, nt) for e in range(nt)]
    sent = []
    scatter = []
    for e in range(nt):
        scatter.append([
            launch(terms_ref.at[peer, peers_t[e]], first.at[d, e], send1.at[d, e],
                   recv1.at[d, e], "batch", peer)
            for d, peer in enumerate(peers_b)
        ])
        sent += scatter[-1]
    across = []
    for e in range(nt):
        total = terms_ref[mine_b, peers_t[e]].astype(jnp.float32)
        for d in range(nb - 1):
            scatter[e][d].wait_recv()
            total = total + first[d, e].astype(jnp.float32)
        if e < nt - 1:
            partial[e] = total.astype(jnp.bfloat16)
            across.append(launch(partial.at[e], second.at[e], send2.at[e], recv2.at[e],
                                 "tiles", peers_t[e]))
    for e in range(nt - 1):
        across[e].wait_recv()
        total = total + second[e].astype(jnp.float32)
    final[...] = total.astype(jnp.bfloat16)

    gather = [
        launch(final, out_ref.at[mine_b, mine_t], send3.at[e], recv3.at[e], "tiles", peers_t[e])
        for e in range(nt - 1)
    ]
    last = [
        launch(final, out_ref.at[mine_b, mine_t], send4.at[d, nt - 1], recv4.at[d, nt - 1],
               "batch", peer)
        for d, peer in enumerate(peers_b)
    ]
    out_ref[mine_b, mine_t] = final[...]
    for e in range(nt - 1):
        gather[e].wait_recv()
        origin = lax.rem(mine_t - 1 - e + nt, nt)
        block = out_ref.at[mine_b, origin]
        last += [
            launch(block, block, send4.at[d, e], recv4.at[d, e], "batch", peer)
            for d, peer in enumerate(peers_b)
        ]
    for copy in last:
        copy.wait_recv()
    for copy in sent + across + gather + last:
        copy.wait_send()


def reduce_all(terms):
    nb, nt, rows, lanes = terms.shape
    dma = pltpu.SemaphoreType.DMA
    return pl.pallas_call(
        functools.partial(reduce_kernel, nb, nt),
        out_shape=jax.ShapeDtypeStruct(terms.shape, jnp.bfloat16),
        in_specs=[pl.BlockSpec(memory_space=pltpu.VMEM)],
        out_specs=pl.BlockSpec(memory_space=pltpu.VMEM),
        scratch_shapes=[
            pltpu.VMEM((nb - 1, nt, rows, lanes), jnp.bfloat16),
            pltpu.VMEM((nt - 1, rows, lanes), jnp.bfloat16),
            pltpu.VMEM((nt - 1, rows, lanes), jnp.bfloat16),
            pltpu.VMEM((rows, lanes), jnp.bfloat16),
            dma((nb - 1, nt)), dma((nb - 1, nt)), dma((nt - 1,)), dma((nt - 1,)),
            dma((nt - 1,)), dma((nt - 1,)), dma((nb - 1, nt)), dma((nb - 1, nt)),
        ],
        compiler_params=pltpu.CompilerParams(collective_id=0, has_side_effects=True),
        name="reduce_all",
    )(terms)


def summed_everywhere(terms):
    nb, nt = lax.axis_size("batch"), lax.axis_size("tiles")
    rows, columns = terms.shape
    pieces = (rows // 16) * (columns // LANES)
    share = -(-pieces // (nb * nt))
    tiled = terms.astype(jnp.bfloat16).reshape(rows // 16, 16, columns // LANES, LANES)
    tiled = tiled.transpose(0, 2, 1, 3).reshape(pieces, 16, LANES)
    tiled = jnp.pad(tiled, ((0, share * nb * nt - pieces), (0, 0), (0, 0)))
    total = reduce_all(tiled.reshape(nb, nt, share * 16, LANES))
    total = total.reshape(share * nb * nt, 16, LANES)[0:pieces]
    total = total.reshape(rows // 16, columns // LANES, 16, LANES).transpose(0, 2, 1, 3)
    return total.reshape(rows, columns).astype(jnp.float32)


def mask_bias(window_rows, sides, present):
    per_slab = GF * GR
    query_tile = jnp.arange(per_slab, dtype=jnp.int32)
    key_local = jnp.tile(query_tile, 3)
    key_side = jnp.repeat(jnp.stack(sides), per_slab)
    here = jnp.repeat(jnp.stack(present), per_slab)
    frame_step = key_local[None, :] // GR - query_tile[:, None] // GR
    row_step = key_local[None, :] % GR - query_tile[:, None] % GR
    code = (key_side[None, :] * 3 + frame_step + 1) * 3 + row_step + 1
    nearby = (jnp.abs(frame_step) <= 1) & (jnp.abs(row_step) <= 1)
    offsets = jnp.arange(27, dtype=jnp.int32)
    listed = jnp.sum(
        jnp.where(code[:, :, None] == offsets[None, None, :], window_rows[:, None, :], 0), axis=2
    )
    allowed = nearby & here[None, :] & (listed > 0)
    return jnp.repeat(jnp.where(allowed, 0.0, -1e30).astype(jnp.float32), TILE, axis=1)


def per_device(
    hidden,
    frozen_queries,
    frozen_keys,
    frozen_values,
    reward_output_gradient,
    truncation_step,
    modulation,
    adapter_down_weight,
    adapter_up_weight,
    window,
):
    slab_rows, width = hidden.shape[1:]
    across = frozen_queries.shape[2]
    rank = adapter_up_weight.shape[1]
    count = lax.axis_size("tiles")
    index = lax.axis_index("tiles")
    even = index % 2 == 0
    down_rows = adapter_down_weight.transpose(0, 2, 1)
    x_low, low, queries, kv = project(
        truncation_step, hidden, modulation, down_rows, adapter_up_weight,
        frozen_queries, frozen_keys, frozen_values,
    )

    zero, one, two = (jnp.int32(i) for i in range(3))
    swap_side = jnp.where(even, two, zero)
    relay_side = jnp.where(even, zero, two)
    relay_here = jnp.where(even, index >= 1, index < count - 1)
    bias = mask_bias(
        window, (one, swap_side, relay_side), (jnp.bool_(True), jnp.bool_(True), relay_here)
    )

    attended, rq_total, owned, ups = attend(
        count, bias, queries, reward_output_gradient, kv, low, adapter_up_weight
    )
    rank_grads = jnp.concatenate([rq_total, owned], axis=0).astype(jnp.bfloat16)
    down_terms = jnp.dot(rank_grads, x_low, preferred_element_type=jnp.float32)
    norm_factor = 1.0 / math.sqrt(
        hidden.shape[0] * lax.axis_size("batch") * slab_rows * count
    )
    terms = jnp.concatenate([down_terms, ups], axis=1) * norm_factor
    total = summed_everywhere(terms)
    grad_down = total[:, 0:width].reshape(3, rank, width).transpose(0, 2, 1)
    grad_up = total[:, width:].reshape(3, rank, across)
    return (attended, grad_down, grad_up)


def solution(mesh):
    placed = (
        P("batch", "tiles", None),
        P("batch", "tiles", None),
        P("batch", "tiles", None),
        P("batch", "tiles", None),
        P("batch", "tiles", None),
        P("batch"),
        P(),
        P(),
        P(),
        P("tiles", None),
    )
    return jax.shard_map(
        per_device,
        mesh=mesh,
        in_specs=placed,
        out_specs=(P("batch", "tiles", None), P(), P()),
        check_vma=False,
    )
```

profile of v0, /device:TPU:1, one launch (start us, length us, event | category | flops | bytes accessed | tf_op | source)
XLA Modules:
  0.0 156.5 jit_solution(11053194264951718153)
XLA Ops:
  1.5 0.1 and.92
  1.7 0.1 mul.31
  1.8 0.1 broadcast_in_dim_tile.8
  2.0 1.0 select_reduce_fusion
  3.1 0.1 copy.17
  3.3 0.6 copy.25
  3.9 12.3 %project.1 = (bf16[512,3072]{1,0:T(8,128)(2,1)}, bf16[512,128]{1,0:T(8,128)(2,1)}, bf16[512,1536]{1,0:T(8,128)(2,1)}, bf16[12,512,256]{2,1,0:T(8,128)(2,1)}) custom-call(s32[1]{0:T(128)S(6)} %copy.27.step_ref, bf16[1,512,3072]{2,1,0:T(8,128)(2,1)} %hidden_ref.1, f32[50,2,3072]{2,1,0:T(2,128)} %mod_ref.1, bf16[3,32,3072]{2,1,0:T(8,128)(2,1)} %bitcast.36, ...), custom_call_target="tpu_custom_call" | custom-call | tf_op jit(solution)/shard_map/project/pallas_call | solution.py:66
  16.1 94.2 %attend.1 = (bf16[1,512,1536]{2,1,0:T(8,128)(2,1)}, f32[32,512]{1,0:T(8,128)}, f32[64,512]{1,0:T(8,128)}, f32[96,1536]{1,0:T(8,128)}) custom-call(f32[4,1536]{1,0:T(4,128)} %bitcast.38, bf16[512,128]{1,0:T(8,128)(2,1)} %get-tuple-element.11.low_ref, bf16[3,32,1536]{2,1,0:T(8,128)(2,1)} %up_ref.3, bf16[512,1536]{1,0:T(8,128)(2,1)} %get-tuple-element.12.q_hbm, ...), custom_call_target="tpu_custom_call" | custom-call | tf_op jit(solution)/shard_map/attend/pallas_call | solution.py:218
  110.3 0.8 convert.9
  111.2 0.9 convert.10
  112.1 0.6 fusion.1
  112.7 0.4 copy-done.2
  113.2 0.1 fusion
  113.3 0.5 convert_element_type.23
  113.8 0.1 copy.18
  113.9 1.1 pad.5
  115.0 36.1 %reduce_all.1 = bf16[4,8,112,128]{3,2,1,0:T(8,128)(2,1)} custom-call(bf16[4,8,112,128]{3,2,1,0:T(8,128)(2,1)} %bitcast.31), custom_call_target="tpu_custom_call" | custom-call | tf_op jit(solution)/shard_map/reduce_all/pallas_call | solution.py:323
  151.1 1.3 slice.12
  152.4 0.2 convert_bitcast_fusion
  152.6 0.6 copy.19
  153.1 0.3 copy.24
  153.4 0.9 slice.14
  154.3 1.1 slice.13
  155.4 1.1 copy.28
  (15 shorter events, 0.6 us)
Async XLA Ops:
  16.1 96.0 %copy-start = (bf16[512,3072]{1,0:T(8,128)(2,1)S(1)}, bf16[512,3072]{1,0:T(8,128)(2,1)}, u32[]{:S(2)}) copy-start(bf16[512,3072]{1,0:T(8,128)(2,1)} %get-tuple-element.17) | copy-start | bytes 9437188
  112.1 1.1 copy-start.2
  153.4 2.0 %copy-start.1 = (bf16[1,512,1536]{2,1,0:T(8,128)(2,1)S(1)}, bf16[1,512,1536]{2,1,0:T(8,128)(2,1)}, u32[]{:S(2)}) copy-start(bf16[1,512,1536]{2,1,0:T(8,128)(2,1)} %get-tuple-element.26) | copy-start | bytes 4718596
where the time goes:
time: 157 us
  Pallas kernels  143 us (91%)
  local copies, waits for them, and re-layouts  8.66 us (6%)
  other arithmetic  3.3 us (2%)
    pallas_call x1, Pallas kernels, attend(): pl.pallas_call(functools.partial(attend_kernel, rank, count), out_shape=[...  94.2 us
    pallas_call x1, Pallas kernels, reduce_all(): pl.pallas_call(functools.partial(reduce_kernel, nb, nt), out_shape=jax.Sh...  36.1 us
    pallas_call x1, Pallas kernels, project(): pl.pallas_call(project_kernel, out_shape=[jax.ShapeDtypeStruct((rows, wid...  12.3 us

commit v1 on v0

v1 whole, which is shorter than its diff:
```python
import functools
import math

import jax
import jax.numpy as jnp
from jax import lax
from jax.experimental import pallas as pl
from jax.experimental.pallas import tpu as pltpu
from jax.sharding import PartitionSpec as P

HEAD = 128
TILE = 128
GF = 2
GR = 2
LANES = 128
ROWS = 16
PARTS = 4
EARLY = 6
AHEAD = 8
BF16 = jnp.bfloat16
F32 = jnp.float32


def dot_nt(a, b):
    return lax.dot_general(
        a, b, (((1,), (1,)), ((), ())), preferred_element_type=jnp.float32
    )


def dot_tn(a, b):
    return lax.dot_general(
        a, b, (((0,), (0,)), ((), ())), preferred_element_type=jnp.float32
    )


def dot_nn(a, b):
    return jnp.dot(a, b, preferred_element_type=jnp.float32)


def remote(src, dst, send, recv, peer):
    return pltpu.make_async_remote_copy(
        src_ref=src, dst_ref=dst, send_sem=send, recv_sem=recv,
        device_id=peer, device_id_type=pl.DeviceIdType.MESH,
    )


class Place:
    def __init__(self, nb, nt):
        self.nb, self.nt = nb, nt
        self.nx, self.nz = nb // 2, nt // 2
        self.nxy = 2 * self.nx
        b, t = lax.axis_index("batch"), lax.axis_index("tiles")
        self.b, self.t = b, t
        self.core, self.x = lax.rem(b, 2), b // 2
        self.y, self.z = lax.rem(t, 2), t // 2

    def core_peer(self):
        return {"batch": self.b + 1 - 2 * self.core}

    def xy_offset(self, d, sign):
        dx, dy = d // 2, d % 2
        x = lax.rem(self.x + sign * dx + self.nx, self.nx)
        return x, lax.rem(self.y + dy, 2)

    def xy_peer(self, d):
        x, y = self.xy_offset(d, 1)
        return {"batch": x * 2 + self.core, "tiles": self.z * 2 + y}

    def xy_index(self, d, sign):
        x, y = self.xy_offset(d, sign)
        return x * 2 + y

    def z_peer(self, e):
        return {"tiles": lax.rem(self.z + e, self.nz) * 2 + self.y}


def share_of(tiles, nb, nt):
    return -(-tiles // (nb * nt))


def sum_shapes(tiles, nb, nt):
    share = share_of(tiles, nb, nt)
    nxy, nz = nb, nt // 2
    quarter = nz * share
    total = nb * nt * share
    dma = pltpu.SemaphoreType.DMA
    return [
        pltpu.VMEM((total, ROWS, LANES), BF16),
        pltpu.VMEM((total // 2, ROWS, LANES), BF16),
        pltpu.VMEM((nxy - 1, quarter, ROWS, LANES), BF16),
        pltpu.VMEM((nxy - 1, quarter, ROWS, LANES), BF16),
        pltpu.VMEM((quarter, ROWS, LANES), F32),
        pltpu.VMEM((nz - 1, share, ROWS, LANES), BF16),
        pltpu.VMEM((nz - 1, share, ROWS, LANES), BF16),
        pltpu.VMEM((total, ROWS, LANES), BF16),
        dma((nxy,)), dma((nxy,)), dma((nxy - 1,)), dma((nxy - 1,)),
        dma((nz - 1,)), dma((nz - 1,)), dma((nz - 1,)), dma((nz - 1,)),
        dma((nxy - 1, nz)), dma((nxy - 1, nz)), dma((nxy, nz)), dma((nxy, nz)),
    ]


class Sum:
    def __init__(self, place, tiles, refs):
        self.place, self.tiles = place, tiles
        (self.terms, self.pair, self.part1, self.got1, self.acc, self.part2, self.got2,
         self.out, self.s0, self.r0, self.s1, self.r1, self.s2, self.r2, self.s3, self.r3,
         self.s4, self.r4, self.s5, self.r5) = refs
        self.share = share_of(tiles, place.nb, place.nt)
        self.quarter = place.nz * self.share
        self.half = place.nxy * self.quarter
        self.mine = place.core * self.half
        self.order = list(range(place.nxy - 1, -1, -1))
        self.sent = []

    def clear(self):
        pad = self.terms.shape[0] - self.tiles
        if pad:
            self.terms[self.tiles:] = jnp.zeros((pad, ROWS, LANES), BF16)

    def go(self, *args):
        copy = remote(*args)
        copy.start()
        self.sent.append(copy)
        return copy

    def pair_start(self):
        p = self.place
        other = (1 - p.core) * self.half
        self.c0 = {}
        for d in self.order:
            q = p.xy_index(d, 1) * self.quarter
            self.c0[d] = self.go(self.terms.at[pl.ds(other + q, self.quarter)],
                                 self.pair.at[pl.ds(q, self.quarter)],
                                 self.s0.at[d], self.r0.at[d], p.core_peer())

    def xy_start(self):
        p = self.place
        self.c1 = {}
        for d in self.order:
            q = p.xy_index(d, 1) * self.quarter
            self.c0[d].wait_recv()
            total = (self.terms[pl.ds(self.mine + q, self.quarter)].astype(F32)
                     + self.pair[pl.ds(q, self.quarter)].astype(F32))
            if d == 0:
                self.acc[...] = total
            else:
                self.part1[d - 1] = total.astype(BF16)
                self.c1[d] = self.go(self.part1.at[d - 1], self.got1.at[d - 1],
                                     self.s1.at[d - 1], self.r1.at[d - 1], p.xy_peer(d))

    def z_start(self):
        p = self.place
        for d in self.order:
            if d:
                self.c1[d].wait_recv()
        total = self.acc[...]
        for d in range(1, p.nxy):
            total = total + self.got1[d - 1].astype(F32)
        self.acc[...] = total
        self.c2 = []
        for e in range(1, p.nz):
            spot = lax.rem(p.z + e, p.nz) * self.share
            self.part2[e - 1] = self.acc[pl.ds(spot, self.share)].astype(BF16)
            self.c2.append(self.go(self.part2.at[e - 1], self.got2.at[e - 1],
                                   self.s2.at[e - 1], self.r2.at[e - 1], p.z_peer(e)))

    def spot(self, d, e):
        p = self.place
        plane = lax.rem(p.z - e + p.nz, p.nz) * self.share
        return self.out.at[pl.ds(self.mine + p.xy_index(d, -1) * self.quarter + plane, self.share)]

    def z_back(self):
        p = self.place
        total = self.acc[pl.ds(p.z * self.share, self.share)]
        for e in range(1, p.nz):
            self.c2[e - 1].wait_recv()
            total = total + self.got2[e - 1].astype(F32)
        mine = self.spot(0, 0)
        mine[...] = total.astype(BF16)
        self.c3 = [self.go(mine, mine, self.s3.at[e - 1], self.r3.at[e - 1], p.z_peer(e))
                   for e in range(1, p.nz)]

    def xy_back(self):
        p = self.place
        self.c4, self.c5 = {}, []
        for e in range(p.nz):
            if e:
                self.c3[e - 1].wait_recv()
            piece = self.spot(0, e)
            for d in self.order:
                if d:
                    self.c4[d, e] = self.go(piece, piece, self.s4.at[d - 1, e],
                                            self.r4.at[d - 1, e], p.xy_peer(d))
            self.c5.append(self.go(piece, piece, self.s5.at[0, e], self.r5.at[0, e],
                                   p.core_peer()))

    def pair_back(self):
        p = self.place
        for e in range(p.nz):
            for d in range(1, p.nxy):
                self.c4[d, e].wait_recv()
                piece = self.spot(d, e)
                self.c5.append(self.go(piece, piece, self.s5.at[d, e], self.r5.at[d, e],
                                       p.core_peer()))

    def finish(self):
        for copy in self.c5:
            copy.wait_recv()

    def drain(self):
        for copy in self.sent:
            copy.wait_send()


def fused_kernel(nb, nt, rank, norm_factor, step_ref, window_ref, hidden_hbm, mod_hbm, down_hbm, up_hbm,
                 fq_hbm, fk_hbm, fv_hbm, g_hbm,
                 att_hbm, gd_ref, gu_ref,
                 x_ref, mod_all, mod_ref, down_ref, up_ref, ups, fq_ref, fk_ref, fv_ref, g_ref,
                 swap_ref, relay_ref, low_ref, low_swap, low_relay, bias_ref, q_ref, kl, vl,
                 probs_s, grad_s, rkv, rq_ref, r_out, r_in, att_ref,
                 load, att_sem, swap_send, swap_recv, relay_send, relay_recv,
                 low_send, low_recv, r_send, r_recv, *sums):
    place = Place(nb, nt)
    t_index, odd = place.t, place.y
    rows, across = fq_ref.shape[1:]
    heads = across // HEAD
    width = x_ref.shape[1]
    half = rows // 2
    chunks = PARTS * heads
    per = len(sums) // 2
    first = Sum(place, (rank // ROWS) * (width // LANES) + (3 * rank // ROWS) * heads, sums[:per])
    later = Sum(place, (2 * rank // ROWS) * (width // LANES), sums[per:])

    partner = {"tiles": t_index + 1 - 2 * odd}
    target = {"tiles": lax.rem(t_index + 2 - 4 * odd + nt, nt)}
    other = {"tiles": lax.rem(t_index - 1 + 2 * odd + nt, nt)}
    even = odd == 0
    relay_in = jnp.where(even, t_index >= 2, t_index < nt - 2)
    relay_out = jnp.where(even, t_index < nt - 2, t_index >= 2)

    blocks = 2 * (rows // TILE)
    block = rows // blocks
    hidden_loads = [
        pltpu.make_async_copy(hidden_hbm.at[0, pl.ds(i * block, block)],
                              x_ref.at[pl.ds(i * block, block)], load.at[i])
        for i in range(blocks)
    ]
    others = [
        pltpu.make_async_copy(src, dst, load.at[blocks + i])
        for i, (src, dst) in enumerate((
            (mod_hbm, mod_all), (down_hbm, down_ref.at[pl.ds(0, 3 * rank)]), (up_hbm, up_ref),
            (fq_hbm, fq_ref), (fk_hbm, fk_ref), (fv_hbm, fv_ref), (g_hbm, g_ref)))
    ]

    barrier = pltpu.get_barrier_semaphore()
    greet = [place.core_peer(), other]
    greet += [place.xy_peer(d) for d in range(1, place.nxy)]
    greet += [place.z_peer(e) for e in range(1, place.nz)]
    for peer in greet:
        pl.semaphore_signal(barrier, inc=1, device_id=peer, device_id_type=pl.DeviceIdType.MESH)
    hidden_loads[0].start()
    for copy in others[:3]:
        copy.start()
    for copy in hidden_loads[1:]:
        copy.start()
    for copy in others[3:]:
        copy.start()

    scale_root = 1.0 / math.sqrt(HEAD)
    scale_two = scale_root * math.log2(math.e)
    per_slab = GF * GR
    sides = (jnp.int32(9), 18 * (1 - odd), 18 * odd)
    for s, side in enumerate(sides):
        for t in range(per_slab):
            for u in range(per_slab):
                code = side + 3 * (u // GR - t // GR + 1) + u % GR - t % GR + 1
                value = jnp.where(window_ref[t, code] > 0, 0.0, -1e30).astype(F32)
                if s == 2:
                    value = jnp.where(relay_in, value, -1e30)
                spot = (s * per_slab + u) * TILE
                bias_ref[t:t + 1, spot:spot + TILE] = jnp.full((1, TILE), value, F32)

    pl.semaphore_wait(barrier, len(greet))

    def swap(h, part):
        src = (fk_hbm, fv_hbm)[part // 2]
        start = (part % 2) * half
        lanes = pl.ds(pl.multiple_of(h * HEAD, HEAD), HEAD)
        c = h * PARTS + part
        return remote(src.at[0, pl.ds(start, half), lanes],
                      swap_ref.at[h, part // 2, pl.ds(start, half)],
                      swap_send.at[c], swap_recv.at[c], partner)

    def chunk(ref, c):
        return ref.at[c // PARTS, lax.rem(c, PARTS) // 2, pl.ds(lax.rem(c, 2) * half, half)]

    def relay(c):
        return remote(chunk(swap_ref, c), chunk(relay_ref, c), relay_send.at[c], relay_recv.at[c],
                      target)

    def pump(c):
        remote(chunk(swap_ref, c), chunk(swap_ref, c), swap_send.at[c], swap_recv.at[c],
               partner).wait_recv()

        @pl.when(relay_out)
        def _():
            relay(c).start()

    for c in range(EARLY):
        swap(c // PARTS, c % PARTS).start()

    @pl.when(jnp.logical_not(relay_in))
    def _():
        low_relay[...] = jnp.zeros_like(low_relay)

        def clear(h, carry):
            relay_ref[h] = jnp.zeros(relay_ref.shape[1:], BF16)
            return carry

        lax.fori_loop(0, heads, clear, 0)
        r_in[1] = jnp.zeros(r_in.shape[1:], BF16)

    first.clear()
    later.clear()
    rq_ref[...] = jnp.zeros_like(rq_ref)
    rkv[...] = jnp.zeros_like(rkv)
    ups[...] = jnp.zeros_like(ups)
    down_ref[3 * rank:] = jnp.zeros((LANES - 3 * rank, width), BF16)

    for copy in others[:3]:
        copy.wait()
    mod_ref[...] = mod_all[step_ref[0]]

    def build(h, carry):
        lanes = pl.ds(pl.multiple_of(h * HEAD, HEAD), HEAD)
        for j in range(3):
            ups[h, j * rank:(j + 1) * rank, j * HEAD:(j + 1) * HEAD] = (
                up_ref[j * rank:(j + 1) * rank, lanes])
        return carry

    lax.fori_loop(0, heads, build, 0)

    def modulate(i, carry):
        span = pl.ds(pl.multiple_of(i * block, block), block)
        pltpu.make_async_copy(hidden_hbm.at[0, span], x_ref.at[span], load.at[i]).wait()
        x = x_ref[span, :].astype(F32)
        mean = jnp.sum(x, axis=1, keepdims=True) * (1.0 / width)
        centred = x - mean
        variance = jnp.sum(centred * centred, axis=1, keepdims=True) * (1.0 / width)
        normed = centred * lax.rsqrt(variance + 1e-06)
        x_low = (normed * (1.0 + mod_ref[1:2, :]) + mod_ref[0:1, :]).astype(BF16)
        x_ref[span, :] = x_low
        low_ref[span, :] = dot_nt(x_low, down_ref[...]).astype(BF16)

        @pl.when(jnp.logical_and(lax.rem(i, 2) == 1, i >= 3))
        def _():
            pump((i - 3) // 2)

        return carry

    lax.fori_loop(0, blocks, modulate, 0)
    pumped = (blocks - 1 - 3) // 2 + 1
    low_first = remote(low_ref, low_swap, low_send.at[0], low_recv.at[0], partner)
    low_next = remote(low_swap, low_relay, low_send.at[1], low_recv.at[1], target)
    low_first.start()
    for c in range(EARLY, 2 * PARTS):
        swap(c // PARTS, c % PARTS).start()

    def send_rest(h, carry):
        for part in range(PARTS):
            swap(h, part).start()
        return carry

    lax.fori_loop(2, heads, send_rest, 0)
    for copy in others[3:]:
        copy.wait()
    for c in range(pumped, EARLY):
        pump(c)
    low_first.wait_recv()

    @pl.when(relay_out)
    def _():
        low_next.start()

    for c in range(EARLY, AHEAD):
        pump(c)

    @pl.when(relay_in)
    def _():
        low_next.wait_recv()

    for s, low in enumerate((low_ref, low_swap, low_relay)):
        kl[s * rows:(s + 1) * rows, HEAD:] = low[...]
        vl[s * rows:(s + 1) * rows, HEAD:] = low[...]

    def reach(h):
        return AHEAD + ((chunks - AHEAD) * h) // (heads - 1)

    up_base = (rank // ROWS) * (width // LANES)

    def att_copy(h):
        lanes = pl.ds(pl.multiple_of(h * HEAD, HEAD), HEAD)
        return pltpu.make_async_copy(att_ref.at[h], att_hbm.at[0, :, lanes], att_sem.at[h])

    def one_head(h, carry):
        @pl.when(relay_in)
        def _():
            for part in range(PARTS):
                relay(h * PARTS + part).wait_recv()

        lanes = pl.ds(pl.multiple_of(h * HEAD, HEAD), HEAD)
        own = dot_nn(low_ref[...], ups[h])
        q_ref[...] = (fq_ref[0, :, lanes].astype(F32) + own[:, 0:HEAD]).astype(BF16)
        kl[0:rows, 0:HEAD] = (fk_ref[0, :, lanes].astype(F32) + own[:, HEAD:2 * HEAD]).astype(BF16)
        vl[0:rows, 0:HEAD] = (fv_ref[0, :, lanes].astype(F32) + own[:, 2 * HEAD:]).astype(BF16)
        for s, (low, part) in enumerate(((low_swap, swap_ref), (low_relay, relay_ref))):
            add = dot_nn(low[...], ups[h, :, HEAD:])
            span = slice((s + 1) * rows, (s + 2) * rows)
            kl[span, 0:HEAD] = (part[h, 0].astype(F32) + add[:, 0:HEAD]).astype(BF16)
            vl[span, 0:HEAD] = (part[h, 1].astype(F32) + add[:, HEAD:]).astype(BF16)
        for t in range(rows // TILE):
            span = slice(t * TILE, (t + 1) * TILE)
            scores = dot_nt(q_ref[span, :], kl[:, 0:HEAD]) * scale_two + bias_ref[t:t + 1, :]
            top = jnp.max(scores, axis=1, keepdims=True)
            weights = jnp.exp2(scores - top)
            inverse = 1.0 / jnp.sum(weights, axis=1, keepdims=True)
            probs = weights * inverse
            prob_grad = dot_nt(g_ref[0, span, lanes], vl[:, 0:HEAD])
            centre = jnp.sum(probs * prob_grad, axis=1, keepdims=True)
            probs_s[span, :] = probs.astype(BF16)
            grad_s[span, :] = (probs * (prob_grad - centre) * scale_root).astype(BF16)
            c = reach(h) + t

            @pl.when(jnp.logical_and(c < reach(h + 1), c < chunks))
            def _():
                pump(c)

        q_all = q_ref[...]
        g_all = g_ref[0, :, lanes]
        q_up = dot_nt(up_ref[rank:2 * rank, lanes], q_all).astype(BF16)
        g_up = dot_nt(up_ref[2 * rank:3 * rank, lanes], g_all).astype(BF16)
        rkv[0:rank, :] += dot_nn(q_up, grad_s[...])
        rkv[rank:2 * rank, :] += dot_nn(g_up, probs_s[...])
        att = dot_nn(probs_s[...], vl[...])
        att_ref[h] = att[:, 0:HEAD].astype(BF16)
        att_copy(h).start()
        low_v = att[:, HEAD:].astype(BF16)
        dq = dot_nn(grad_s[...], kl[...])
        dq_low = dq[:, 0:HEAD].astype(BF16)
        low_k = dq[:, HEAD:].astype(BF16)
        rq_ref[...] += dot_nt(up_ref[0:rank, lanes], dq_low)
        ups_terms = (dot_tn(low_ref[...], dq_low), dot_tn(low_k, q_all), dot_tn(low_v, g_all))
        for j, term in enumerate(ups_terms):
            for r in range(rank // ROWS):
                start = j * rank + r * ROWS
                spot = up_base + h * (3 * rank // ROWS) + start // ROWS
                first.terms[spot] = (term[start:start + ROWS] * norm_factor).astype(BF16)
        return carry

    lax.fori_loop(0, heads, one_head, 0)

    returns = []
    for s, peer in enumerate((partner, other)):
        r_out[s] = rkv[:, (s + 1) * rows:(s + 2) * rows].astype(BF16)
        returns.append(remote(r_out.at[s], r_in.at[s], r_send.at[s], r_recv.at[s], peer))
    returns[0].start()

    @pl.when(relay_in)
    def _():
        returns[1].start()

    def down_dot(total, grads, count):
        def columns(i, carry):
            lanes = pl.ds(pl.multiple_of(i * 2 * LANES, 2 * LANES), 2 * LANES)
            term = dot_nn(grads, x_ref[:, lanes]) * norm_factor
            for l in range(2):
                for r in range(count):
                    total.terms[(i * 2 + l) * count + r] = (
                        term[r * ROWS:(r + 1) * ROWS, l * LANES:(l + 1) * LANES].astype(BF16))
            return carry

        lax.fori_loop(0, width // (2 * LANES), columns, 0)

    down_dot(first, rq_ref[...].astype(BF16), rank // ROWS)
    first.pair_start()
    returns[0].wait_recv()

    @pl.when(relay_in)
    def _():
        returns[1].wait_recv()

    owned = rkv[:, 0:rows] + r_in[0].astype(F32) + r_in[1].astype(F32)
    down_dot(later, owned.astype(BF16), 2 * rank // ROWS)
    later.pair_start()
    first.xy_start()
    later.xy_start()
    first.z_start()
    later.z_start()
    first.z_back()
    later.z_back()
    first.xy_back()
    later.xy_back()
    first.pair_back()
    later.pair_back()
    first.finish()

    def unpack_first(i, carry):
        lanes = pl.ds(pl.multiple_of(i * LANES, LANES), LANES)
        for r in range(rank // ROWS):
            gd_ref[r * ROWS:(r + 1) * ROWS, lanes] = first.out[i * (rank // ROWS) + r]
        return carry

    lax.fori_loop(0, width // LANES, unpack_first, 0)

    def unpack_up(h, carry):
        lanes = pl.ds(pl.multiple_of(h * LANES, LANES), LANES)
        for r in range(3 * rank // ROWS):
            gu_ref[r * ROWS:(r + 1) * ROWS, lanes] = first.out[up_base + h * (3 * rank // ROWS) + r]
        return carry

    lax.fori_loop(0, heads, unpack_up, 0)
    later.finish()

    def unpack_later(i, carry):
        lanes = pl.ds(pl.multiple_of(i * LANES, LANES), LANES)
        for r in range(2 * rank // ROWS):
            gd_ref[rank + r * ROWS:rank + (r + 1) * ROWS, lanes] = (
                later.out[i * (2 * rank // ROWS) + r])
        return carry

    lax.fori_loop(0, width // LANES, unpack_later, 0)

    low_first.wait_send()

    @pl.when(relay_out)
    def _():
        low_next.wait_send()

    def swap_sent(h, carry):
        for part in range(PARTS):
            swap(h, part).wait_send()
        return carry

    lax.fori_loop(0, heads, swap_sent, 0)

    @pl.when(relay_out)
    def _():
        lax.fori_loop(0, chunks, lambda c, carry: (relay(c).wait_send(), carry)[1], 0)

    returns[0].wait_send()

    @pl.when(relay_in)
    def _():
        returns[1].wait_send()

    lax.fori_loop(0, heads, lambda h, carry: (att_copy(h).wait(), carry)[1], 0)
    first.drain()
    later.drain()


def fused(nb, nt, norm_factor, step, window, hidden, modulation, down, up, fq, fk, fv, g):
    _, rows, width = hidden.shape
    across = fq.shape[2]
    heads = across // HEAD
    rank = up.shape[0] // 3
    dma = pltpu.SemaphoreType.DMA
    vmem = pltpu.VMEM
    smem = pl.BlockSpec(memory_space=pltpu.SMEM)
    anywhere = pl.BlockSpec(memory_space=pl.ANY)
    whole = pl.BlockSpec(memory_space=pltpu.VMEM)
    chunks = PARTS * heads
    blocks = 2 * (rows // TILE)
    first_tiles = (rank // ROWS) * (width // LANES) + (3 * rank // ROWS) * heads
    later_tiles = (2 * rank // ROWS) * (width // LANES)
    return pl.pallas_call(
        functools.partial(fused_kernel, nb, nt, rank, norm_factor),
        out_shape=[
            jax.ShapeDtypeStruct((1, rows, across), BF16),
            jax.ShapeDtypeStruct((3 * rank, width), BF16),
            jax.ShapeDtypeStruct((3 * rank, across), BF16),
        ],
        in_specs=[smem, smem] + [anywhere] * 8,
        out_specs=[anywhere, whole, whole],
        scratch_shapes=[
            vmem((rows, width), BF16), vmem(modulation.shape, F32), vmem((2, width), F32),
            vmem((LANES, width), BF16), vmem(up.shape, BF16), vmem((heads, LANES, 3 * HEAD), BF16),
            vmem(fq.shape, BF16), vmem(fq.shape, BF16), vmem(fq.shape, BF16), vmem(fq.shape, BF16),
            vmem((heads, 2, rows, HEAD), BF16), vmem((heads, 2, rows, HEAD), BF16),
            vmem((rows, LANES), BF16), vmem((rows, LANES), BF16), vmem((rows, LANES), BF16),
            vmem((8, 3 * rows), F32), vmem((rows, HEAD), BF16),
            vmem((3 * rows, 2 * HEAD), BF16), vmem((3 * rows, 2 * HEAD), BF16),
            vmem((rows, 3 * rows), BF16), vmem((rows, 3 * rows), BF16),
            vmem((2 * rank, 3 * rows), F32), vmem((rank, rows), F32),
            vmem((2, 2 * rank, rows), BF16), vmem((2, 2 * rank, rows), BF16),
            vmem((heads, rows, HEAD), BF16),
            dma((blocks + 7,)), dma((heads,)),
            dma((chunks,)), dma((chunks,)), dma((chunks,)), dma((chunks,)),
            dma((2,)), dma((2,)), dma((2,)), dma((2,)),
        ] + sum_shapes(first_tiles, nb, nt) + sum_shapes(later_tiles, nb, nt),
        compiler_params=pltpu.CompilerParams(
            collective_id=0, has_side_effects=True, vmem_limit_bytes=60 << 20
        ),
        name="fused",
    )(step, window, hidden, modulation, down, up, fq, fk, fv, g)


def per_device(
    hidden,
    frozen_queries,
    frozen_keys,
    frozen_values,
    reward_output_gradient,
    truncation_step,
    modulation,
    adapter_down_weight,
    adapter_up_weight,
    window,
):
    slab_rows, width = hidden.shape[1:]
    across = frozen_queries.shape[2]
    rank = adapter_up_weight.shape[1]
    nb, nt = lax.axis_size("batch"), lax.axis_size("tiles")
    norm_factor = 1.0 / math.sqrt(hidden.shape[0] * nb * slab_rows * nt)
    down = adapter_down_weight.transpose(0, 2, 1).reshape(3 * rank, width)
    up = adapter_up_weight.reshape(3 * rank, across)
    attended, grad_down, grad_up = fused(
        nb, nt, norm_factor, truncation_step, window, hidden, modulation, down, up,
        frozen_queries, frozen_keys, frozen_values, reward_output_gradient,
    )
    grad_down = grad_down.astype(jnp.float32).reshape(3, rank, width).transpose(0, 2, 1)
    grad_up = grad_up.astype(jnp.float32).reshape(3, rank, across)
    return (attended, grad_down, grad_up)


def solution(mesh):
    placed = (
        P("batch", "tiles", None),
        P("batch", "tiles", None),
        P("batch", "tiles", None),
        P("batch", "tiles", None),
        P("batch", "tiles", None),
        P("batch"),
        P(),
        P(),
        P(),
        P("tiles", None),
    )
    return jax.shard_map(
        per_device,
        mesh=mesh,
        in_specs=placed,
        out_specs=(P("batch", "tiles", None), P(), P()),
        check_vma=False,
    )
```

time: 157 us -> 127 us (0.81)
  Pallas kernels: 143 us -> 120 us
  local copies, waits for them, and re-layouts: 8.66 us -> 1.15 us
    pallas_call x3 -> x1, Pallas kernels: 143 us -> 120 us  [fused(): pl.pallas_call(functools.partial(fused_kernel, nb, nt, rank, norm_factor)...]
    slice x3 -> x0, local copies, waits for them, and re-layouts: 3.27 us -> none  [the longest x1 1.32 us: summed_everywhere(): total = total.reshape(share * nb * nt, 16, LANES)[0:pieces]]
    transpose x0 -> x1, other arithmetic: none -> 2.3 us  [per_device(): grad_down.astype(jnp.float32).reshape(3, rank, width).transpose(0, 2, 1)]
    reshape x0 -> x1, other arithmetic: none -> 1.83 us  [per_device(): grad_up = grad_up.astype(jnp.float32).reshape(3, rank, across)]
    another operation x2 -> x0, other arithmetic: 1.76 us -> none
where the time goes in v1:
time: 127 us
  Pallas kernels  120 us (94%)
  other arithmetic  4.12 us (3%)
  between operations  1.3 us (1%)
    pallas_call x1, Pallas kernels, fused(): pl.pallas_call(functools.partial(fused_kernel, nb, nt, rank, norm_factor)...  120 us

profile of v1, /device:TPU:1, one launch (start us, length us, event | category | flops | bytes accessed | tf_op | source)
XLA Modules:
  0.0 126.6 jit_solution(6147138141920115716)
XLA Ops:
  1.3 120.0 %fused.1 = (bf16[1,512,1536]{2,1,0:T(8,128)(2,1)}, bf16[96,3072]{1,0:T(8,128)(2,1)}, bf16[96,1536]{1,0:T(8,128)(2,1)}) custom-call(s32[1]{0:T(128)S(6)} %copy.14.step_ref, s32[4,27]{1,0:T(4,128)} %window_ref.1, bf16[1,512,3072]{2,1,0:T(8,128)(2,1)} %hidden_hbm.1, f32[50,2,3072]{2,1,0:T(2,128)} %mod_hbm.1, bf16[96,3072]{1,0:T(8,128)(2,1)} %bitcast.10, ...), custom_call_target="tpu_custom_call" | custom-call | tf_op jit(solution)/shard_map/fused/pallas_call | solution.py:575
  121.3 0.0 copy-start
  121.3 2.3 %convert_bitcast_fusion = f32[3,3072,32]{1,2,0:T(8,128)} fusion(bf16[3,32,3072]{2,1,0:T(8,128)(2,1)} %bitcast.11), kind=kLoop, calls=%fused_computation | loop fusion | flops 294912 | bytes 1769472 | tf_op jit(solution)/shard_map/transpose | solution.py:630
  123.6 1.8 %convert.4 = f32[3,32,1536]{2,1,0:T(8,128)} convert(bf16[3,32,1536]{2,1,0:T(8,128)(2,1)} %bitcast.13) | non-fusion elementwise | flops 147456 | bytes 884736 | tf_op jit(solution)/shard_map/reshape | solution.py:631
  125.5 0.0 copy-done
  125.5 1.1 copy.15
Async XLA Ops:
  121.3 4.1 %copy-start = (bf16[1,512,1536]{2,1,0:T(8,128)(2,1)S(1)}, bf16[1,512,1536]{2,1,0:T(8,128)(2,1)}, u32[]{:S(2)}) copy-start(bf16[1,512,1536]{2,1,0:T(8,128)(2,1)} %get-tuple-element.12) | copy-start | bytes 4718596

commit v2 on v1

--- a/solution.py
+++ b/solution.py
@@ -15,8 +15,7 @@
 LANES = 128
 ROWS = 16
 PARTS = 4
-EARLY = 6
-AHEAD = 8
+EARLY = 4
 BF16 = jnp.bfloat16
 F32 = jnp.float32
 
@@ -216,7 +215,7 @@
                  fq_hbm, fk_hbm, fv_hbm, g_hbm,
                  att_hbm, gd_ref, gu_ref,
                  x_ref, mod_all, mod_ref, down_ref, up_ref, ups, fq_ref, fk_ref, fv_ref, g_ref,
-                 swap_ref, relay_ref, low_ref, low_swap, low_relay, bias_ref, q_ref, kl, vl,
+                 swap_ref, relay_ref, low_pack, low_got, low_ref, low_swap, low_relay, bias_ref, q_ref, kl, vl,
                  probs_s, grad_s, rkv, rq_ref, r_out, r_in, att_ref,
                  load, att_sem, swap_send, swap_recv, relay_send, relay_recv,
                  low_send, low_recv, r_send, r_recv, *sums):
@@ -248,7 +247,10 @@
     others = [
         pltpu.make_async_copy(src, dst, load.at[blocks + i])
         for i, (src, dst) in enumerate((
-            (mod_hbm, mod_all), (down_hbm, down_ref.at[pl.ds(0, 3 * rank)]), (up_hbm, up_ref),
+            (mod_hbm, mod_all), (down_hbm, down_ref.at[pl.ds(0, 3 * rank)]),
+            (down_hbm.at[pl.ds(rank, 2 * rank)], down_ref.at[pl.ds(LANES, 2 * rank)]),
+            (down_hbm.at[pl.ds(rank, 2 * rank)], down_ref.at[pl.ds(LANES + 2 * rank, 2 * rank)]),
+            (up_hbm, up_ref),
             (fq_hbm, fq_ref), (fk_hbm, fk_ref), (fv_hbm, fv_ref), (g_hbm, g_ref)))
     ]
 
@@ -259,11 +261,11 @@
     for peer in greet:
         pl.semaphore_signal(barrier, inc=1, device_id=peer, device_id_type=pl.DeviceIdType.MESH)
     hidden_loads[0].start()
-    for copy in others[:3]:
+    for copy in others[:4]:
         copy.start()
     for copy in hidden_loads[1:]:
         copy.start()
-    for copy in others[3:]:
+    for copy in others[4:]:
         copy.start()
 
     scale_root = 1.0 / math.sqrt(HEAD)
@@ -325,20 +327,18 @@
     rq_ref[...] = jnp.zeros_like(rq_ref)
     rkv[...] = jnp.zeros_like(rkv)
     ups[...] = jnp.zeros_like(ups)
-    down_ref[3 * rank:] = jnp.zeros((LANES - 3 * rank, width), BF16)
-
-    for copy in others[:3]:
+    down_ref[3 * rank:LANES] = jnp.zeros((LANES - 3 * rank, width), BF16)
+
+    for copy in others[:4]:
         copy.wait()
     mod_ref[...] = mod_all[step_ref[0]]
 
-    def build(h, carry):
-        lanes = pl.ds(pl.multiple_of(h * HEAD, HEAD), HEAD)
-        for j in range(3):
-            ups[h, j * rank:(j + 1) * rank, j * HEAD:(j + 1) * HEAD] = (
-                up_ref[j * rank:(j + 1) * rank, lanes])
-        return carry
-
-    lax.fori_loop(0, heads, build, 0)
+    def low_copy(g):
+        return remote(low_pack.at[g], low_got.at[g], low_send.at[g], low_recv.at[g], partner)
+
+    def low_next(g):
+        return remote(low_got.at[g], low_got.at[2 + g], low_send.at[2 + g], low_recv.at[2 + g],
+                      target)
 
     def modulate(i, carry):
         span = pl.ds(pl.multiple_of(i * block, block), block)
@@ -350,19 +350,27 @@
         normed = centred * lax.rsqrt(variance + 1e-06)
         x_low = (normed * (1.0 + mod_ref[1:2, :]) + mod_ref[0:1, :]).astype(BF16)
         x_ref[span, :] = x_low
-        low_ref[span, :] = dot_nt(x_low, down_ref[...]).astype(BF16)
-
-        @pl.when(jnp.logical_and(lax.rem(i, 2) == 1, i >= 3))
+        low = dot_nt(x_low, down_ref[...]).astype(BF16)
+        low_ref[span, :] = low[:, 0:LANES]
+        inner = pl.ds(pl.multiple_of(lax.rem(i, blocks // 4) * block, block), block)
+        group = i // (blocks // 2)
+        second = lax.rem(i // (blocks // 4), 2) == 1
+
+        @pl.when(jnp.logical_not(second))
         def _():
-            pump((i - 3) // 2)
+            low_pack[group, inner, 0:2 * rank] = low[:, LANES:LANES + 2 * rank]
+
+        @pl.when(second)
+        def _():
+            low_pack[group, inner, 2 * rank:] = low[:, LANES + 2 * rank:]
+
+        @pl.when(lax.rem(i, blocks // 2) == blocks // 2 - 1)
+        def _():
+            low_copy(group).start()
 
         return carry
 
     lax.fori_loop(0, blocks, modulate, 0)
-    pumped = (blocks - 1 - 3) // 2 + 1
-    low_first = remote(low_ref, low_swap, low_send.at[0], low_recv.at[0], partner)
-    low_next = remote(low_swap, low_relay, low_send.at[1], low_recv.at[1], target)
-    low_first.start()
     for c in range(EARLY, 2 * PARTS):
         swap(c // PARTS, c % PARTS).start()
 
@@ -372,37 +380,68 @@
         return carry
 
     lax.fori_loop(2, heads, send_rest, 0)
-    for copy in others[3:]:
+    pump(0)
+    pump(1)
+    for copy in others[4:]:
         copy.wait()
-    for c in range(pumped, EARLY):
-        pump(c)
-    low_first.wait_recv()
-
-    @pl.when(relay_out)
-    def _():
-        low_next.start()
-
-    for c in range(EARLY, AHEAD):
-        pump(c)
+
+    def build(h, carry):
+        lanes = pl.ds(pl.multiple_of(h * HEAD, HEAD), HEAD)
+        for j in range(3):
+            ups[h, j * rank:(j + 1) * rank, j * HEAD:(j + 1) * HEAD] = (
+                up_ref[j * rank:(j + 1) * rank, lanes])
+        return carry
+
+    lax.fori_loop(0, heads, build, 0)
+    pump(2)
+    pump(3)
+    for g in range(2):
+        low_copy(g).wait_recv()
+
+        @pl.when(relay_out)
+        def _(g=g):
+            low_next(g).start()
+
+    row = lax.broadcasted_iota(jnp.int32, (LANES, LANES), 0)
+    lane = lax.broadcasted_iota(jnp.int32, (LANES, LANES), 1)
+    inside = jnp.logical_and(lane >= rank, lane < 3 * rank)
+
+    def unpack_low(s, dst):
+        quarter = rows // 4
+        for part in range(2):
+            pick = jnp.logical_and(inside, row == lane - rank + part * 2 * rank)
+            select = jnp.where(pick, 1.0, 0.0).astype(BF16)
+            for g in range(2):
+                start = (2 * g + part) * quarter
+                dst[start:start + quarter, :] = dot_nn(low_got[2 * s + g], select).astype(BF16)
+
+    unpack_low(0, low_swap)
 
     @pl.when(relay_in)
     def _():
-        low_next.wait_recv()
+        for g in range(2):
+            low_next(g).wait_recv()
+        unpack_low(1, low_relay)
 
     for s, low in enumerate((low_ref, low_swap, low_relay)):
         kl[s * rows:(s + 1) * rows, HEAD:] = low[...]
         vl[s * rows:(s + 1) * rows, HEAD:] = low[...]
 
-    def reach(h):
-        return AHEAD + ((chunks - AHEAD) * h) // (heads - 1)
-
     up_base = (rank // ROWS) * (width // LANES)
 
     def att_copy(h):
         lanes = pl.ds(pl.multiple_of(h * HEAD, HEAD), HEAD)
         return pltpu.make_async_copy(att_ref.at[h], att_hbm.at[0, :, lanes], att_sem.at[h])
 
+    def pump_next(h, part):
+        @pl.when(h + 1 < heads)
+        def _():
+            pump((h + 1) * PARTS + part)
+
     def one_head(h, carry):
+        pump_next(h, 0)
+        pump_next(h, 1)
+
         @pl.when(relay_in)
         def _():
             for part in range(PARTS):
@@ -429,11 +468,8 @@
             centre = jnp.sum(probs * prob_grad, axis=1, keepdims=True)
             probs_s[span, :] = probs.astype(BF16)
             grad_s[span, :] = (probs * (prob_grad - centre) * scale_root).astype(BF16)
-            c = reach(h) + t
-
-            @pl.when(jnp.logical_and(c < reach(h + 1), c < chunks))
-            def _():
-                pump(c)
+            if t % 2 == 0:
+                pump_next(h, 2 + t // 2)
 
         q_all = q_ref[...]
         g_all = g_ref[0, :, lanes]
@@ -507,7 +543,7 @@
     def unpack_first(i, carry):
         lanes = pl.ds(pl.multiple_of(i * LANES, LANES), LANES)
         for r in range(rank // ROWS):
-            gd_ref[r * ROWS:(r + 1) * ROWS, lanes] = first.out[i * (rank // ROWS) + r]
+            gd_ref[r * ROWS:(r + 1) * ROWS, lanes] = first.out[i * (rank // ROWS) + r].astype(F32)
         return carry
 
     lax.fori_loop(0, width // LANES, unpack_first, 0)
@@ -515,7 +551,8 @@
     def unpack_up(h, carry):
         lanes = pl.ds(pl.multiple_of(h * LANES, LANES), LANES)
         for r in range(3 * rank // ROWS):
-            gu_ref[r * ROWS:(r + 1) * ROWS, lanes] = first.out[up_base + h * (3 * rank // ROWS) + r]
+            gu_ref[r * ROWS:(r + 1) * ROWS, lanes] = (
+                first.out[up_base + h * (3 * rank // ROWS) + r].astype(F32))
         return carry
 
     lax.fori_loop(0, heads, unpack_up, 0)
@@ -525,16 +562,18 @@
         lanes = pl.ds(pl.multiple_of(i * LANES, LANES), LANES)
         for r in range(2 * rank // ROWS):
             gd_ref[rank + r * ROWS:rank + (r + 1) * ROWS, lanes] = (
-                later.out[i * (2 * rank // ROWS) + r])
+                later.out[i * (2 * rank // ROWS) + r].astype(F32))
         return carry
 
     lax.fori_loop(0, width // LANES, unpack_later, 0)
 
-    low_first.wait_send()
+    for g in range(2):
+        low_copy(g).wait_send()
 
     @pl.when(relay_out)
     def _():
-        low_next.wait_send()
+        for g in range(2):
+            low_next(g).wait_send()
 
     def swap_sent(h, carry):
         for part in range(PARTS):
@@ -576,16 +615,17 @@
         functools.partial(fused_kernel, nb, nt, rank, norm_factor),
         out_shape=[
             jax.ShapeDtypeStruct((1, rows, across), BF16),
-            jax.ShapeDtypeStruct((3 * rank, width), BF16),
-            jax.ShapeDtypeStruct((3 * rank, across), BF16),
+            jax.ShapeDtypeStruct((3 * rank, width), F32),
+            jax.ShapeDtypeStruct((3 * rank, across), F32),
         ],
         in_specs=[smem, smem] + [anywhere] * 8,
         out_specs=[anywhere, whole, whole],
         scratch_shapes=[
             vmem((rows, width), BF16), vmem(modulation.shape, F32), vmem((2, width), F32),
-            vmem((LANES, width), BF16), vmem(up.shape, BF16), vmem((heads, LANES, 3 * HEAD), BF16),
+            vmem((LANES + 4 * rank, width), BF16), vmem(up.shape, BF16), vmem((heads, LANES, 3 * HEAD), BF16),
             vmem(fq.shape, BF16), vmem(fq.shape, BF16), vmem(fq.shape, BF16), vmem(fq.shape, BF16),
             vmem((heads, 2, rows, HEAD), BF16), vmem((heads, 2, rows, HEAD), BF16),
+            vmem((2, rows // 4, LANES), BF16), vmem((4, rows // 4, LANES), BF16),
             vmem((rows, LANES), BF16), vmem((rows, LANES), BF16), vmem((rows, LANES), BF16),
             vmem((8, 3 * rows), F32), vmem((rows, HEAD), BF16),
             vmem((3 * rows, 2 * HEAD), BF16), vmem((3 * rows, 2 * HEAD), BF16),
@@ -593,9 +633,9 @@
             vmem((2 * rank, 3 * rows), F32), vmem((rank, rows), F32),
             vmem((2, 2 * rank, rows), BF16), vmem((2, 2 * rank, rows), BF16),
             vmem((heads, rows, HEAD), BF16),
-            dma((blocks + 7,)), dma((heads,)),
+            dma((blocks + 9,)), dma((heads,)),
             dma((chunks,)), dma((chunks,)), dma((chunks,)), dma((chunks,)),
-            dma((2,)), dma((2,)), dma((2,)), dma((2,)),
+            dma((4,)), dma((4,)), dma((2,)), dma((2,)),
         ] + sum_shapes(first_tiles, nb, nt) + sum_shapes(later_tiles, nb, nt),
         compiler_params=pltpu.CompilerParams(
             collective_id=0, has_side_effects=True, vmem_limit_bytes=60 << 20
@@ -627,8 +667,8 @@
         nb, nt, norm_factor, truncation_step, window, hidden, modulation, down, up,
         frozen_queries, frozen_keys, frozen_values, reward_output_gradient,
     )
-    grad_down = grad_down.astype(jnp.float32).reshape(3, rank, width).transpose(0, 2, 1)
-    grad_up = grad_up.astype(jnp.float32).reshape(3, rank, across)
+    grad_down = grad_down.reshape(3, rank, width).transpose(0, 2, 1)
+    grad_up = grad_up.reshape(3, rank, across)
     return (attended, grad_down, grad_up)
 
 

time: 127 us -> 129 us (1.016)
  other arithmetic: 4.12 us -> 0 us
  local copies, waits for them, and re-layouts: 1.15 us -> 5.03 us
  Pallas kernels: 120 us -> 122 us
    unnamed x3 -> x7, local copies, waits for them, and re-layouts: 1.15 us -> 5.03 us
    transpose x1 -> x0, other arithmetic: 2.3 us -> none  [per_device(): grad_down.astype(jnp.float32).reshape(3, rank, width).transpose(0, 2, 1)]
    pallas_call x1, Pallas kernels: 120 us -> 122 us  [fused(): pl.pallas_call(functools.partial(fused_kernel, nb, nt, rank, norm_factor)...]
    reshape x1 -> x0, other arithmetic: 1.83 us -> none  [per_device(): grad_up = grad_up.astype(jnp.float32).reshape(3, rank, across)]
where the time goes in v2:
time: 129 us; the launch traced here: 128 us
  Pallas kernels  122 us (95%)
  local copies, waits for them, and re-layouts  5.03 us (4%)
  between operations  1.3 us (1%)
    pallas_call x1, Pallas kernels, fused(): pl.pallas_call(functools.partial(fused_kernel, nb, nt, rank, norm_factor)...  122 us
    unnamed x7, local copies, waits for them, and re-layouts  5.03 us

profile of v2, /device:TPU:1, one launch (start us, length us, event | category | flops | bytes accessed | tf_op | source)
XLA Modules:
  0.0 128.3 jit_solution(3976684747645577224)
XLA Ops:
  1.3 122.0 %fused.1 = (bf16[1,512,1536]{2,1,0:T(8,128)(2,1)}, f32[96,3072]{1,0:T(8,128)}, f32[96,1536]{1,0:T(8,128)}) custom-call(s32[1]{0:T(128)S(6)} %copy.16.step_ref, s32[4,27]{1,0:T(4,128)} %window_ref.1, bf16[1,512,3072]{2,1,0:T(8,128)(2,1)} %hidden_hbm.1, f32[50,2,3072]{2,1,0:T(2,128)} %mod_hbm.1, bf16[96,3072]{1,0:T(8,128)(2,1)} %bitcast.9, ...), custom_call_target="tpu_custom_call" | custom-call | tf_op jit(solution)/shard_map/fused/pallas_call | solution.py:614
  123.3 0.0 copy-start
  123.3 2.7 %copy.17 = bf16[1,512,1536]{2,1,0:T(8,128)(2,1)} copy(bf16[1,512,1536]{2,1,0:T(8,128)(2,1)} %get-tuple-element.12) | data formatting | bytes 3145728
  126.0 0.0 copy-done
  126.0 0.0 copy-start.1
  126.0 1.0 copy.18
  127.0 0.5 copy-done.1
  127.5 0.8 copy.19
Async XLA Ops:
  123.3 2.8 %copy-start = (f32[96,3072]{1,0:T(8,128)S(1)}, f32[96,3072]{1,0:T(8,128)}, u32[]{:S(2)}) copy-start(f32[96,3072]{1,0:T(8,128)} %get-tuple-element.7) | copy-start | bytes 3538948
  126.0 1.5 %copy-start.1 = (f32[96,1536]{1,0:T(8,128)S(1)}, f32[96,1536]{1,0:T(8,128)}, u32[]{:S(2)}) copy-start(f32[96,1536]{1,0:T(8,128)} %get-tuple-element.8) | copy-start | bytes 1769476

commit v3 on v2

--- a/solution.py
+++ b/solution.py
@@ -15,7 +15,7 @@
 LANES = 128
 ROWS = 16
 PARTS = 4
-EARLY = 4
+EARLY = 5
 BF16 = jnp.bfloat16
 F32 = jnp.float32
 
@@ -75,6 +75,13 @@
 
 def share_of(tiles, nb, nt):
     return -(-tiles // (nb * nt))
+
+
+def split_tiles(rank, width, heads, nb, nt):
+    one = (rank // ROWS) * (width // LANES)
+    ups = (3 * rank // ROWS) * heads
+    spare = min(ups, share_of(one, nb, nt) * nb * nt - one)
+    return 2 * one + ups - spare, one + spare
 
 
 def sum_shapes(tiles, nb, nt):
@@ -91,7 +98,6 @@
         pltpu.VMEM((quarter, ROWS, LANES), F32),
         pltpu.VMEM((nz - 1, share, ROWS, LANES), BF16),
         pltpu.VMEM((nz - 1, share, ROWS, LANES), BF16),
-        pltpu.VMEM((total, ROWS, LANES), BF16),
         dma((nxy,)), dma((nxy,)), dma((nxy - 1,)), dma((nxy - 1,)),
         dma((nz - 1,)), dma((nz - 1,)), dma((nz - 1,)), dma((nz - 1,)),
         dma((nxy - 1, nz)), dma((nxy - 1, nz)), dma((nxy, nz)), dma((nxy, nz)),
@@ -99,10 +105,10 @@
 
 
 class Sum:
-    def __init__(self, place, tiles, refs):
-        self.place, self.tiles = place, tiles
+    def __init__(self, place, tiles, out, refs):
+        self.place, self.tiles, self.out = place, tiles, out
         (self.terms, self.pair, self.part1, self.got1, self.acc, self.part2, self.got2,
-         self.out, self.s0, self.r0, self.s1, self.r1, self.s2, self.r2, self.s3, self.r3,
+         self.s0, self.r0, self.s1, self.r1, self.s2, self.r2, self.s3, self.r3,
          self.s4, self.r4, self.s5, self.r5) = refs
         self.share = share_of(tiles, place.nb, place.nt)
         self.quarter = place.nz * self.share
@@ -213,10 +219,10 @@
 
 def fused_kernel(nb, nt, rank, norm_factor, step_ref, window_ref, hidden_hbm, mod_hbm, down_hbm, up_hbm,
                  fq_hbm, fk_hbm, fv_hbm, g_hbm,
-                 att_hbm, gd_ref, gu_ref,
+                 att_hbm, first_out, later_out,
                  x_ref, mod_all, mod_ref, down_ref, up_ref, ups, fq_ref, fk_ref, fv_ref, g_ref,
                  swap_ref, relay_ref, low_pack, low_got, low_ref, low_swap, low_relay, bias_ref, q_ref, kl, vl,
-                 probs_s, grad_s, rkv, rq_ref, r_out, r_in, att_ref,
+                 probs_f, probs_s, grad_s, rkv, rq_ref, r_out, r_in, att_ref, up_terms,
                  load, att_sem, swap_send, swap_recv, relay_send, relay_recv,
                  low_send, low_recv, r_send, r_recv, *sums):
     place = Place(nb, nt)
@@ -227,8 +233,9 @@
     half = rows // 2
     chunks = PARTS * heads
     per = len(sums) // 2
-    first = Sum(place, (rank // ROWS) * (width // LANES) + (3 * rank // ROWS) * heads, sums[:per])
-    later = Sum(place, (2 * rank // ROWS) * (width // LANES), sums[per:])
+    first_tiles, later_tiles = split_tiles(rank, width, heads, nb, nt)
+    first = Sum(place, first_tiles, first_out, sums[:per])
+    later = Sum(place, later_tiles, later_out, sums[per:])
 
     partner = {"tiles": t_index + 1 - 2 * odd}
     target = {"tiles": lax.rem(t_index + 2 - 4 * odd + nt, nt)}
@@ -237,8 +244,8 @@
     relay_in = jnp.where(even, t_index >= 2, t_index < nt - 2)
     relay_out = jnp.where(even, t_index < nt - 2, t_index >= 2)
 
-    blocks = 2 * (rows // TILE)
-    block = rows // blocks
+    blocks = rows // TILE
+    block = TILE
     hidden_loads = [
         pltpu.make_async_copy(hidden_hbm.at[0, pl.ds(i * block, block)],
                               x_ref.at[pl.ds(i * block, block)], load.at[i])
@@ -248,8 +255,6 @@
         pltpu.make_async_copy(src, dst, load.at[blocks + i])
         for i, (src, dst) in enumerate((
             (mod_hbm, mod_all), (down_hbm, down_ref.at[pl.ds(0, 3 * rank)]),
-            (down_hbm.at[pl.ds(rank, 2 * rank)], down_ref.at[pl.ds(LANES, 2 * rank)]),
-            (down_hbm.at[pl.ds(rank, 2 * rank)], down_ref.at[pl.ds(LANES + 2 * rank, 2 * rank)]),
             (up_hbm, up_ref),
             (fq_hbm, fq_ref), (fk_hbm, fk_ref), (fv_hbm, fv_ref), (g_hbm, g_ref)))
     ]
@@ -261,11 +266,9 @@
     for peer in greet:
         pl.semaphore_signal(barrier, inc=1, device_id=peer, device_id_type=pl.DeviceIdType.MESH)
     hidden_loads[0].start()
-    for copy in others[:4]:
+    for copy in others[:2]:
         copy.start()
     for copy in hidden_loads[1:]:
-        copy.start()
-    for copy in others[4:]:
         copy.start()
 
     scale_root = 1.0 / math.sqrt(HEAD)
@@ -320,7 +323,8 @@
             return carry
 
         lax.fori_loop(0, heads, clear, 0)
-        r_in[1] = jnp.zeros(r_in.shape[1:], BF16)
+        for j in range(2):
+            r_in[2 * j + 1] = jnp.zeros(r_in.shape[1:], BF16)
 
     first.clear()
     later.clear()
@@ -329,9 +333,12 @@
     ups[...] = jnp.zeros_like(ups)
     down_ref[3 * rank:LANES] = jnp.zeros((LANES - 3 * rank, width), BF16)
 
-    for copy in others[:4]:
+    for copy in others[:2]:
         copy.wait()
     mod_ref[...] = mod_all[step_ref[0]]
+    row = lax.broadcasted_iota(jnp.int32, (LANES, LANES), 0)
+    lane = lax.broadcasted_iota(jnp.int32, (LANES, LANES), 1)
+    wide = 2 * rank
 
     def low_copy(g):
         return remote(low_pack.at[g], low_got.at[g], low_send.at[g], low_recv.at[g], partner)
@@ -339,6 +346,18 @@
     def low_next(g):
         return remote(low_got.at[g], low_got.at[2 + g], low_send.at[2 + g], low_recv.at[2 + g],
                       target)
+
+    def one_hot(pick):
+        return jnp.where(pick, 1.0, 0.0).astype(BF16)
+
+    def pack_low(g):
+        total = jnp.zeros((rows // 4, LANES), F32)
+        for part in range(2):
+            pick = jnp.logical_and(lane // wide == part, row - rank == lane - part * wide)
+            start = (2 * g + part) * (rows // 4)
+            total = total + dot_nn(low_ref[start:start + rows // 4, :], one_hot(pick))
+        low_pack[g] = total.astype(BF16)
+        low_copy(g).start()
 
     def modulate(i, carry):
         span = pl.ds(pl.multiple_of(i * block, block), block)
@@ -350,27 +369,16 @@
         normed = centred * lax.rsqrt(variance + 1e-06)
         x_low = (normed * (1.0 + mod_ref[1:2, :]) + mod_ref[0:1, :]).astype(BF16)
         x_ref[span, :] = x_low
-        low = dot_nt(x_low, down_ref[...]).astype(BF16)
-        low_ref[span, :] = low[:, 0:LANES]
-        inner = pl.ds(pl.multiple_of(lax.rem(i, blocks // 4) * block, block), block)
-        group = i // (blocks // 2)
-        second = lax.rem(i // (blocks // 4), 2) == 1
-
-        @pl.when(jnp.logical_not(second))
-        def _():
-            low_pack[group, inner, 0:2 * rank] = low[:, LANES:LANES + 2 * rank]
-
-        @pl.when(second)
-        def _():
-            low_pack[group, inner, 2 * rank:] = low[:, LANES + 2 * rank:]
-
-        @pl.when(lax.rem(i, blocks // 2) == blocks // 2 - 1)
-        def _():
-            low_copy(group).start()
-
+        low_ref[span, :] = dot_nt(x_low, down_ref[...]).astype(BF16)
         return carry
 
-    lax.fori_loop(0, blocks, modulate, 0)
+    half_blocks = blocks // 2
+    lax.fori_loop(0, half_blocks, modulate, 0)
+    pack_low(0)
+    lax.fori_loop(half_blocks, blocks - 1, modulate, 0)
+    pump(0)
+    lax.fori_loop(blocks - 1, blocks, modulate, 0)
+    pack_low(1)
     for c in range(EARLY, 2 * PARTS):
         swap(c // PARTS, c % PARTS).start()
 
@@ -380,9 +388,10 @@
         return carry
 
     lax.fori_loop(2, heads, send_rest, 0)
-    pump(0)
+    for copy in others[2:]:
+        copy.start()
     pump(1)
-    for copy in others[4:]:
+    for copy in others[2:]:
         copy.wait()
 
     def build(h, carry):
@@ -402,15 +411,13 @@
         def _(g=g):
             low_next(g).start()
 
-    row = lax.broadcasted_iota(jnp.int32, (LANES, LANES), 0)
-    lane = lax.broadcasted_iota(jnp.int32, (LANES, LANES), 1)
     inside = jnp.logical_and(lane >= rank, lane < 3 * rank)
 
     def unpack_low(s, dst):
         quarter = rows // 4
         for part in range(2):
-            pick = jnp.logical_and(inside, row == lane - rank + part * 2 * rank)
-            select = jnp.where(pick, 1.0, 0.0).astype(BF16)
+            pick = jnp.logical_and(inside, row == lane - rank + part * wide)
+            select = one_hot(pick)
             for g in range(2):
                 start = (2 * g + part) * quarter
                 dst[start:start + quarter, :] = dot_nn(low_got[2 * s + g], select).astype(BF16)
@@ -423,11 +430,38 @@
             low_next(g).wait_recv()
         unpack_low(1, low_relay)
 
+    def value_return(s):
+        return remote(r_out.at[s], r_in.at[s], r_send.at[s], r_recv.at[s], (partner, other)[s])
+
+    def key_return(s):
+        return remote(r_out.at[2 + s], r_in.at[2 + s], r_send.at[2 + s], r_recv.at[2 + s],
+                      (partner, other)[s])
+
+    def send_back(ready, start):
+        base = 0 if ready is value_return else 2
+        for s in range(2):
+            r_out[base + s] = rkv[start:start + rank, (s + 1) * rows:(s + 2) * rows].astype(BF16)
+        ready(0).start()
+
+        @pl.when(relay_in)
+        def _():
+            ready(1).start()
+
+    def take_back(ready, start):
+        base = 0 if ready is value_return else 2
+        ready(0).wait_recv()
+
+        @pl.when(relay_in)
+        def _():
+            ready(1).wait_recv()
+
+        return (rkv[start:start + rank, 0:rows] + r_in[base].astype(F32)
+                + r_in[base + 1].astype(F32)).astype(BF16)
+
     for s, low in enumerate((low_ref, low_swap, low_relay)):
         kl[s * rows:(s + 1) * rows, HEAD:] = low[...]
         vl[s * rows:(s + 1) * rows, HEAD:] = low[...]
 
-    up_base = (rank // ROWS) * (width // LANES)
 
     def att_copy(h):
         lanes = pl.ds(pl.multiple_of(h * HEAD, HEAD), HEAD)
@@ -438,25 +472,29 @@
         def _():
             pump((h + 1) * PARTS + part)
 
-    def one_head(h, carry):
-        pump_next(h, 0)
-        pump_next(h, 1)
-
+    def arrive(h, part):
         @pl.when(relay_in)
         def _():
-            for part in range(PARTS):
-                relay(h * PARTS + part).wait_recv()
-
+            for i in range(2):
+                relay(h * PARTS + 2 * part + i).wait_recv()
+
+    def one_head(h, carry):
         lanes = pl.ds(pl.multiple_of(h * HEAD, HEAD), HEAD)
         own = dot_nn(low_ref[...], ups[h])
         q_ref[...] = (fq_ref[0, :, lanes].astype(F32) + own[:, 0:HEAD]).astype(BF16)
         kl[0:rows, 0:HEAD] = (fk_ref[0, :, lanes].astype(F32) + own[:, HEAD:2 * HEAD]).astype(BF16)
         vl[0:rows, 0:HEAD] = (fv_ref[0, :, lanes].astype(F32) + own[:, 2 * HEAD:]).astype(BF16)
-        for s, (low, part) in enumerate(((low_swap, swap_ref), (low_relay, relay_ref))):
-            add = dot_nn(low[...], ups[h, :, HEAD:])
-            span = slice((s + 1) * rows, (s + 2) * rows)
-            kl[span, 0:HEAD] = (part[h, 0].astype(F32) + add[:, 0:HEAD]).astype(BF16)
-            vl[span, 0:HEAD] = (part[h, 1].astype(F32) + add[:, HEAD:]).astype(BF16)
+        g_up = dot_nt(up_ref[2 * rank:3 * rank, lanes], g_ref[0, :, lanes]).astype(BF16)
+        q_up = dot_nt(up_ref[rank:2 * rank, lanes], q_ref[...]).astype(BF16)
+
+        def rebuild(dst, part):
+            for s, (low, got) in enumerate(((low_swap, swap_ref), (low_relay, relay_ref))):
+                add = dot_nn(low[...], ups[h, :, (part + 1) * HEAD:(part + 2) * HEAD])
+                dst[(s + 1) * rows:(s + 2) * rows, 0:HEAD] = (
+                    got[h, part].astype(F32) + add).astype(BF16)
+
+        arrive(h, 0)
+        rebuild(kl, 0)
         for t in range(rows // TILE):
             span = slice(t * TILE, (t + 1) * TILE)
             scores = dot_nt(q_ref[span, :], kl[:, 0:HEAD]) * scale_two + bias_ref[t:t + 1, :]
@@ -464,46 +502,53 @@
             weights = jnp.exp2(scores - top)
             inverse = 1.0 / jnp.sum(weights, axis=1, keepdims=True)
             probs = weights * inverse
+            probs_f[span, :] = probs
+            probs_s[span, :] = probs.astype(BF16)
+            if t == rows // TILE // 2:
+                pump_next(h, 0)
+        rkv[rank:2 * rank, :] += dot_nn(g_up, probs_s[...])
+
+        @pl.when(h == heads - 1)
+        def _():
+            send_back(value_return, rank)
+
+        pump_next(h, 1)
+        arrive(h, 1)
+        rebuild(vl, 1)
+        for t in range(rows // TILE):
+            span = slice(t * TILE, (t + 1) * TILE)
             prob_grad = dot_nt(g_ref[0, span, lanes], vl[:, 0:HEAD])
+            probs = probs_f[span, :]
             centre = jnp.sum(probs * prob_grad, axis=1, keepdims=True)
-            probs_s[span, :] = probs.astype(BF16)
             grad_s[span, :] = (probs * (prob_grad - centre) * scale_root).astype(BF16)
-            if t % 2 == 0:
-                pump_next(h, 2 + t // 2)
+            if t == rows // TILE // 2:
+                pump_next(h, 2)
+        rkv[0:rank, :] += dot_nn(q_up, grad_s[...])
+
+        @pl.when(h == heads - 1)
+        def _():
+            send_back(key_return, 0)
 
         q_all = q_ref[...]
         g_all = g_ref[0, :, lanes]
-        q_up = dot_nt(up_ref[rank:2 * rank, lanes], q_all).astype(BF16)
-        g_up = dot_nt(up_ref[2 * rank:3 * rank, lanes], g_all).astype(BF16)
-        rkv[0:rank, :] += dot_nn(q_up, grad_s[...])
-        rkv[rank:2 * rank, :] += dot_nn(g_up, probs_s[...])
+        dq = dot_nn(grad_s[...], kl[...])
+        dq_low = dq[:, 0:HEAD].astype(BF16)
+        low_k = dq[:, HEAD:].astype(BF16)
+        rq_ref[...] += dot_nt(up_ref[0:rank, lanes], dq_low)
         att = dot_nn(probs_s[...], vl[...])
         att_ref[h] = att[:, 0:HEAD].astype(BF16)
         att_copy(h).start()
         low_v = att[:, HEAD:].astype(BF16)
-        dq = dot_nn(grad_s[...], kl[...])
-        dq_low = dq[:, 0:HEAD].astype(BF16)
-        low_k = dq[:, HEAD:].astype(BF16)
-        rq_ref[...] += dot_nt(up_ref[0:rank, lanes], dq_low)
         ups_terms = (dot_tn(low_ref[...], dq_low), dot_tn(low_k, q_all), dot_tn(low_v, g_all))
         for j, term in enumerate(ups_terms):
             for r in range(rank // ROWS):
                 start = j * rank + r * ROWS
-                spot = up_base + h * (3 * rank // ROWS) + start // ROWS
-                first.terms[spot] = (term[start:start + ROWS] * norm_factor).astype(BF16)
+                spot = h * (3 * rank // ROWS) + start // ROWS
+                up_terms[spot] = (term[start:start + ROWS] * norm_factor).astype(BF16)
+        pump_next(h, 3)
         return carry
 
     lax.fori_loop(0, heads, one_head, 0)
-
-    returns = []
-    for s, peer in enumerate((partner, other)):
-        r_out[s] = rkv[:, (s + 1) * rows:(s + 2) * rows].astype(BF16)
-        returns.append(remote(r_out.at[s], r_in.at[s], r_send.at[s], r_recv.at[s], peer))
-    returns[0].start()
-
-    @pl.when(relay_in)
-    def _():
-        returns[1].start()
 
     def down_dot(total, grads, count):
         def columns(i, carry):
@@ -517,16 +562,17 @@
 
         lax.fori_loop(0, width // (2 * LANES), columns, 0)
 
-    down_dot(first, rq_ref[...].astype(BF16), rank // ROWS)
+    one = (rank // ROWS) * (width // LANES)
+    kept = first_tiles - 2 * one
+    if kept:
+        first.terms[2 * one:first_tiles] = up_terms[0:kept]
+    if later_tiles > one:
+        later.terms[one:later_tiles] = up_terms[kept:]
+    grads = jnp.concatenate([rq_ref[...].astype(BF16), take_back(value_return, rank)], axis=0)
+    down_dot(first, grads, 2 * rank // ROWS)
     first.pair_start()
-    returns[0].wait_recv()
-
-    @pl.when(relay_in)
-    def _():
-        returns[1].wait_recv()
-
-    owned = rkv[:, 0:rows] + r_in[0].astype(F32) + r_in[1].astype(F32)
-    down_dot(later, owned.astype(BF16), 2 * rank // ROWS)
+    grads = take_back(key_return, 0)
+    down_dot(later, grads, rank // ROWS)
     later.pair_start()
     first.xy_start()
     later.xy_start()
@@ -539,33 +585,7 @@
     first.pair_back()
     later.pair_back()
     first.finish()
-
-    def unpack_first(i, carry):
-        lanes = pl.ds(pl.multiple_of(i * LANES, LANES), LANES)
-        for r in range(rank // ROWS):
-            gd_ref[r * ROWS:(r + 1) * ROWS, lanes] = first.out[i * (rank // ROWS) + r].astype(F32)
-        return carry
-
-    lax.fori_loop(0, width // LANES, unpack_first, 0)
-
-    def unpack_up(h, carry):
-        lanes = pl.ds(pl.multiple_of(h * LANES, LANES), LANES)
-        for r in range(3 * rank // ROWS):
-            gu_ref[r * ROWS:(r + 1) * ROWS, lanes] = (
-                first.out[up_base + h * (3 * rank // ROWS) + r].astype(F32))
-        return carry
-
-    lax.fori_loop(0, heads, unpack_up, 0)
     later.finish()
-
-    def unpack_later(i, carry):
-        lanes = pl.ds(pl.multiple_of(i * LANES, LANES), LANES)
-        for r in range(2 * rank // ROWS):
-            gd_ref[rank + r * ROWS:rank + (r + 1) * ROWS, lanes] = (
-                later.out[i * (2 * rank // ROWS) + r].astype(F32))
-        return carry
-
-    lax.fori_loop(0, width // LANES, unpack_later, 0)
 
     for g in range(2):
         low_copy(g).wait_send()
@@ -586,11 +606,13 @@
     def _():
         lax.fori_loop(0, chunks, lambda c, carry: (relay(c).wait_send(), carry)[1], 0)
 
-    returns[0].wait_send()
+    for ready in (value_return, key_return):
+        ready(0).wait_send()
 
     @pl.when(relay_in)
     def _():
-        returns[1].wait_send()
+        for ready in (value_return, key_return):
+            ready(1).wait_send()
 
     lax.fori_loop(0, heads, lambda h, carry: (att_copy(h).wait(), carry)[1], 0)
     first.drain()
@@ -608,40 +630,112 @@
     anywhere = pl.BlockSpec(memory_space=pl.ANY)
     whole = pl.BlockSpec(memory_space=pltpu.VMEM)
     chunks = PARTS * heads
-    blocks = 2 * (rows // TILE)
-    first_tiles = (rank // ROWS) * (width // LANES) + (3 * rank // ROWS) * heads
-    later_tiles = (2 * rank // ROWS) * (width // LANES)
+    blocks = rows // TILE
+    first_tiles, later_tiles = split_tiles(rank, width, heads, nb, nt)
+    totals = [share_of(tiles, nb, nt) * nb * nt for tiles in (first_tiles, later_tiles)]
     return pl.pallas_call(
         functools.partial(fused_kernel, nb, nt, rank, norm_factor),
         out_shape=[
             jax.ShapeDtypeStruct((1, rows, across), BF16),
-            jax.ShapeDtypeStruct((3 * rank, width), F32),
-            jax.ShapeDtypeStruct((3 * rank, across), F32),
+            jax.ShapeDtypeStruct((totals[0], ROWS, LANES), BF16),
+            jax.ShapeDtypeStruct((totals[1], ROWS, LANES), BF16),
         ],
         in_specs=[smem, smem] + [anywhere] * 8,
         out_specs=[anywhere, whole, whole],
         scratch_shapes=[
             vmem((rows, width), BF16), vmem(modulation.shape, F32), vmem((2, width), F32),
-            vmem((LANES + 4 * rank, width), BF16), vmem(up.shape, BF16), vmem((heads, LANES, 3 * HEAD), BF16),
+            vmem((LANES, width), BF16), vmem(up.shape, BF16), vmem((heads, LANES, 3 * HEAD), BF16),
             vmem(fq.shape, BF16), vmem(fq.shape, BF16), vmem(fq.shape, BF16), vmem(fq.shape, BF16),
             vmem((heads, 2, rows, HEAD), BF16), vmem((heads, 2, rows, HEAD), BF16),
             vmem((2, rows // 4, LANES), BF16), vmem((4, rows // 4, LANES), BF16),
             vmem((rows, LANES), BF16), vmem((rows, LANES), BF16), vmem((rows, LANES), BF16),
             vmem((8, 3 * rows), F32), vmem((rows, HEAD), BF16),
             vmem((3 * rows, 2 * HEAD), BF16), vmem((3 * rows, 2 * HEAD), BF16),
+            vmem((rows, 3 * rows), F32),
             vmem((rows, 3 * rows), BF16), vmem((rows, 3 * rows), BF16),
             vmem((2 * rank, 3 * rows), F32), vmem((rank, rows), F32),
-            vmem((2, 2 * rank, rows), BF16), vmem((2, 2 * rank, rows), BF16),
-            vmem((heads, rows, HEAD), BF16),
-            dma((blocks + 9,)), dma((heads,)),
+            vmem((4, rank, rows), BF16), vmem((4, rank, rows), BF16),
+            vmem((heads, rows, HEAD), BF16), vmem((heads * (3 * rank // ROWS), ROWS, LANES), BF16),
+            dma((blocks + 7,)), dma((heads,)),
             dma((chunks,)), dma((chunks,)), dma((chunks,)), dma((chunks,)),
-            dma((4,)), dma((4,)), dma((2,)), dma((2,)),
+            dma((4,)), dma((4,)), dma((4,)), dma((4,)),
         ] + sum_shapes(first_tiles, nb, nt) + sum_shapes(later_tiles, nb, nt),
         compiler_params=pltpu.CompilerParams(
             collective_id=0, has_side_effects=True, vmem_limit_bytes=60 << 20
         ),
         name="fused",
     )(step, window, hidden, modulation, down, up, fq, fk, fv, g)
+
+
+def place_kernel(rank, att_hbm, first_hbm, later_hbm, att_out, down_out, up_out,
+                 att_ref, first_ref, later_ref, down_ref, up_ref, load, store):
+    rows, across = att_ref.shape[1:]
+    heads = across // HEAD
+    width = down_ref.shape[1]
+    one = (rank // ROWS) * (width // LANES)
+    parts = 4
+    cut = rows // parts
+    takes = [pltpu.make_async_copy(first_hbm, first_ref, load.at[0]),
+             pltpu.make_async_copy(later_hbm, later_ref, load.at[1])]
+    moves = [(pltpu.make_async_copy(att_hbm.at[:, pl.ds(i * cut, cut)],
+                                    att_ref.at[:, pl.ds(i * cut, cut)], load.at[2 + i]),
+              pltpu.make_async_copy(att_ref.at[:, pl.ds(i * cut, cut)],
+                                    att_out.at[:, pl.ds(i * cut, cut)], store.at[2 + i]))
+             for i in range(parts)]
+    for copy in takes:
+        copy.start()
+    for copy, _ in moves:
+        copy.start()
+    for copy in takes:
+        copy.wait()
+    step = rank // ROWS
+    for l in range(width // LANES):
+        lanes = slice(l * LANES, (l + 1) * LANES)
+        for r in range(step):
+            spots = (first_ref[l * 2 * step + r], later_ref[l * step + r],
+                     first_ref[l * 2 * step + step + r])
+            for j, tile in enumerate(spots):
+                down_ref[j * rank + r * ROWS:j * rank + (r + 1) * ROWS, lanes] = tile.astype(F32)
+    down_store = pltpu.make_async_copy(down_ref, down_out, store.at[0])
+    down_store.start()
+    spare = min(3 * step * heads, later_ref.shape[0] - one)
+    kept = 3 * step * heads - spare
+    for h in range(heads):
+        lanes = slice(h * HEAD, (h + 1) * HEAD)
+        for r in range(3 * step):
+            k = h * 3 * step + r
+            tile = first_ref[2 * one + k] if k < kept else later_ref[one + k - kept]
+            up_ref[r * ROWS:(r + 1) * ROWS, lanes] = tile.astype(F32)
+    up_store = pltpu.make_async_copy(up_ref, up_out, store.at[1])
+    up_store.start()
+    for copy, then in moves:
+        copy.wait()
+        then.start()
+    for _, then in moves:
+        then.wait()
+    down_store.wait()
+    up_store.wait()
+
+
+def put_in_place(rank, width, attended, first, later):
+    across = attended.shape[2]
+    vmem, dma = pltpu.VMEM, pltpu.SemaphoreType.DMA
+    anywhere = pl.BlockSpec(memory_space=pl.ANY)
+    return pl.pallas_call(
+        functools.partial(place_kernel, rank),
+        out_shape=[
+            jax.ShapeDtypeStruct(attended.shape, BF16),
+            jax.ShapeDtypeStruct((3 * rank, width), F32),
+            jax.ShapeDtypeStruct((3 * rank, across), F32),
+        ],
+        in_specs=[anywhere] * 3,
+        out_specs=[anywhere] * 3,
+        scratch_shapes=[
+            vmem(attended.shape, BF16), vmem(first.shape, BF16), vmem(later.shape, BF16),
+            vmem((3 * rank, width), F32), vmem((3 * rank, across), F32), dma((6,)), dma((6,)),
+        ],
+        name="place",
+    )(attended, first, later)
 
 
 def per_device(
@@ -663,10 +757,11 @@
     norm_factor = 1.0 / math.sqrt(hidden.shape[0] * nb * slab_rows * nt)
     down = adapter_down_weight.transpose(0, 2, 1).reshape(3 * rank, width)
     up = adapter_up_weight.reshape(3 * rank, across)
-    attended, grad_down, grad_up = fused(
+    attended, first, later = fused(
         nb, nt, norm_factor, truncation_step, window, hidden, modulation, down, up,
         frozen_queries, frozen_keys, frozen_values, reward_output_gradient,
     )
+    attended, grad_down, grad_up = put_in_place(rank, width, attended, first, later)
     grad_down = grad_down.reshape(3, rank, width).transpose(0, 2, 1)
     grad_up = grad_up.reshape(3, rank, across)
     return (attended, grad_down, grad_up)

time: 129 us -> 131 us (1.016)
  Pallas kernels: 122 us -> 129 us
  local copies, waits for them, and re-layouts: 5.03 us -> 0 us
    unnamed x7 -> x0, local copies, waits for them, and re-layouts: 5.03 us -> none
    pallas_call x1, Pallas kernels: 122 us -> 126 us  [fused(): pl.pallas_call(functools.partial(fused_kernel, nb, nt, rank, norm_factor)...]
    pallas_call x0 -> x1, Pallas kernels: none -> 3.07 us  [put_in_place(): pl.pallas_call(functools.partial(place_kernel, rank), out_shape=[jax.Shap...]
where the time goes in v3:
time: 131 us; the launch traced here: 130 us
  Pallas kernels  129 us (98%)
    pallas_call x1, Pallas kernels, fused(): pl.pallas_call(functools.partial(fused_kernel, nb, nt, rank, norm_factor)...  126 us
    pallas_call x1, Pallas kernels, put_in_place(): pl.pallas_call(functools.partial(place_kernel, rank), out_shape=[jax.Shap...  3.07 us

profile of v3, /device:TPU:1, one launch (start us, length us, event | category | flops | bytes accessed | tf_op | source)
XLA Modules:
  0.0 130.5 jit_solution(7230532821015067896)
XLA Ops:
  1.3 126.1 %fused.1 = (bf16[1,512,1536]{2,1,0:T(8,128)(2,1)}, bf16[160,16,128]{2,1,0:T(8,128)(2,1)}, bf16[64,16,128]{2,1,0:T(8,128)(2,1)}) custom-call(s32[1]{0:T(128)S(6)} %copy.13.step_ref, s32[4,27]{1,0:T(4,128)} %window_ref.1, bf16[1,512,3072]{2,1,0:T(8,128)(2,1)} %hidden_hbm.1, f32[50,2,3072]{2,1,0:T(2,128)} %mod_hbm.1, bf16[96,3072]{1,0:T(8,128)(2,1)} %bitcast.8, ...), custom_call_target="tpu_custom_call" | custom-call | tf_op jit(solution)/shard_map/fused/pallas_call | solution.py:636
  127.4 3.1 %place.1 = (bf16[1,512,1536]{2,1,0:T(8,128)(2,1)}, f32[96,3072]{1,0:T(8,128)}, f32[96,1536]{1,0:T(8,128)}) custom-call(bf16[1,512,1536]{2,1,0:T(8,128)(2,1)} %get-tuple-element.9.att_hbm, bf16[160,16,128]{2,1,0:T(8,128)(2,1)} %get-tuple-element.10.first_hbm, bf16[64,16,128]{2,1,0:T(8,128)(2,1)} %get-tuple-element.11.later_hbm), custom_call_target="tpu_custom_call" | custom-call | tf_op jit(solution)/shard_map/place/pallas_call | solution.py:724

commit v4 on v3

--- a/solution.py
+++ b/solution.py
@@ -15,7 +15,8 @@
 LANES = 128
 ROWS = 16
 PARTS = 4
-EARLY = 5
+EARLY = 4
+AHEAD = 7
 BF16 = jnp.bfloat16
 F32 = jnp.float32
 
@@ -222,7 +223,7 @@
                  att_hbm, first_out, later_out,
                  x_ref, mod_all, mod_ref, down_ref, up_ref, ups, fq_ref, fk_ref, fv_ref, g_ref,
                  swap_ref, relay_ref, low_pack, low_got, low_ref, low_swap, low_relay, bias_ref, q_ref, kl, vl,
-                 probs_f, probs_s, grad_s, rkv, rq_ref, r_out, r_in, att_ref, up_terms,
+                 probs_s, grad_s, rkv, rq_ref, r_out, r_in, att_ref, up_terms,
                  load, att_sem, swap_send, swap_recv, relay_send, relay_recv,
                  low_send, low_recv, r_send, r_recv, *sums):
     place = Place(nb, nt)
@@ -423,6 +424,8 @@
                 dst[start:start + quarter, :] = dot_nn(low_got[2 * s + g], select).astype(BF16)
 
     unpack_low(0, low_swap)
+    for c in range(PARTS, AHEAD):
+        pump(c)
 
     @pl.when(relay_in)
     def _():
@@ -468,9 +471,11 @@
         return pltpu.make_async_copy(att_ref.at[h], att_hbm.at[0, :, lanes], att_sem.at[h])
 
     def pump_next(h, part):
-        @pl.when(h + 1 < heads)
+        c = h * PARTS + AHEAD + part
+
+        @pl.when(c < chunks)
         def _():
-            pump((h + 1) * PARTS + part)
+            pump(c)
 
     def arrive(h, part):
         @pl.when(relay_in)
@@ -484,17 +489,14 @@
         q_ref[...] = (fq_ref[0, :, lanes].astype(F32) + own[:, 0:HEAD]).astype(BF16)
         kl[0:rows, 0:HEAD] = (fk_ref[0, :, lanes].astype(F32) + own[:, HEAD:2 * HEAD]).astype(BF16)
         vl[0:rows, 0:HEAD] = (fv_ref[0, :, lanes].astype(F32) + own[:, 2 * HEAD:]).astype(BF16)
-        g_up = dot_nt(up_ref[2 * rank:3 * rank, lanes], g_ref[0, :, lanes]).astype(BF16)
-        q_up = dot_nt(up_ref[rank:2 * rank, lanes], q_ref[...]).astype(BF16)
-
-        def rebuild(dst, part):
-            for s, (low, got) in enumerate(((low_swap, swap_ref), (low_relay, relay_ref))):
-                add = dot_nn(low[...], ups[h, :, (part + 1) * HEAD:(part + 2) * HEAD])
-                dst[(s + 1) * rows:(s + 2) * rows, 0:HEAD] = (
-                    got[h, part].astype(F32) + add).astype(BF16)
 
         arrive(h, 0)
-        rebuild(kl, 0)
+        arrive(h, 1)
+        for s, (low, got) in enumerate(((low_swap, swap_ref), (low_relay, relay_ref))):
+            add = dot_nn(low[...], ups[h, :, HEAD:])
+            span = slice((s + 1) * rows, (s + 2) * rows)
+            kl[span, 0:HEAD] = (got[h, 0].astype(F32) + add[:, 0:HEAD]).astype(BF16)
+            vl[span, 0:HEAD] = (got[h, 1].astype(F32) + add[:, HEAD:]).astype(BF16)
         for t in range(rows // TILE):
             span = slice(t * TILE, (t + 1) * TILE)
             scores = dot_nt(q_ref[span, :], kl[:, 0:HEAD]) * scale_two + bias_ref[t:t + 1, :]
@@ -502,53 +504,40 @@
             weights = jnp.exp2(scores - top)
             inverse = 1.0 / jnp.sum(weights, axis=1, keepdims=True)
             probs = weights * inverse
-            probs_f[span, :] = probs
+            prob_grad = dot_nt(g_ref[0, span, lanes], vl[:, 0:HEAD])
+            centre = jnp.sum(probs * prob_grad, axis=1, keepdims=True)
             probs_s[span, :] = probs.astype(BF16)
-            if t == rows // TILE // 2:
+            grad_s[span, :] = (probs * (prob_grad - centre) * scale_root).astype(BF16)
+            if t == 1:
                 pump_next(h, 0)
-        rkv[rank:2 * rank, :] += dot_nn(g_up, probs_s[...])
-
-        @pl.when(h == heads - 1)
-        def _():
-            send_back(value_return, rank)
-
         pump_next(h, 1)
-        arrive(h, 1)
-        rebuild(vl, 1)
-        for t in range(rows // TILE):
-            span = slice(t * TILE, (t + 1) * TILE)
-            prob_grad = dot_nt(g_ref[0, span, lanes], vl[:, 0:HEAD])
-            probs = probs_f[span, :]
-            centre = jnp.sum(probs * prob_grad, axis=1, keepdims=True)
-            grad_s[span, :] = (probs * (prob_grad - centre) * scale_root).astype(BF16)
-            if t == rows // TILE // 2:
-                pump_next(h, 2)
-        rkv[0:rank, :] += dot_nn(q_up, grad_s[...])
-
-        @pl.when(h == heads - 1)
-        def _():
-            send_back(key_return, 0)
-
         q_all = q_ref[...]
         g_all = g_ref[0, :, lanes]
+        q_up = dot_nt(up_ref[rank:2 * rank, lanes], q_all).astype(BF16)
+        g_up = dot_nt(up_ref[2 * rank:3 * rank, lanes], g_all).astype(BF16)
+        rkv[0:rank, :] += dot_nn(q_up, grad_s[...])
+        rkv[rank:2 * rank, :] += dot_nn(g_up, probs_s[...])
+        att = dot_nn(probs_s[...], vl[...])
+        att_ref[h] = att[:, 0:HEAD].astype(BF16)
+        att_copy(h).start()
+        low_v = att[:, HEAD:].astype(BF16)
         dq = dot_nn(grad_s[...], kl[...])
         dq_low = dq[:, 0:HEAD].astype(BF16)
         low_k = dq[:, HEAD:].astype(BF16)
         rq_ref[...] += dot_nt(up_ref[0:rank, lanes], dq_low)
-        att = dot_nn(probs_s[...], vl[...])
-        att_ref[h] = att[:, 0:HEAD].astype(BF16)
-        att_copy(h).start()
-        low_v = att[:, HEAD:].astype(BF16)
         ups_terms = (dot_tn(low_ref[...], dq_low), dot_tn(low_k, q_all), dot_tn(low_v, g_all))
         for j, term in enumerate(ups_terms):
             for r in range(rank // ROWS):
                 start = j * rank + r * ROWS
                 spot = h * (3 * rank // ROWS) + start // ROWS
                 up_terms[spot] = (term[start:start + ROWS] * norm_factor).astype(BF16)
+        pump_next(h, 2)
         pump_next(h, 3)
         return carry
 
     lax.fori_loop(0, heads, one_head, 0)
+    send_back(value_return, rank)
+    send_back(key_return, 0)
 
     def down_dot(total, grads, count):
         def columns(i, carry):
@@ -651,7 +640,6 @@
             vmem((rows, LANES), BF16), vmem((rows, LANES), BF16), vmem((rows, LANES), BF16),
             vmem((8, 3 * rows), F32), vmem((rows, HEAD), BF16),
             vmem((3 * rows, 2 * HEAD), BF16), vmem((3 * rows, 2 * HEAD), BF16),
-            vmem((rows, 3 * rows), F32),
             vmem((rows, 3 * rows), BF16), vmem((rows, 3 * rows), BF16),
             vmem((2 * rank, 3 * rows), F32), vmem((rank, rows), F32),
             vmem((4, rank, rows), BF16), vmem((4, rank, rows), BF16),

time: 131 us -> 123 us (0.939)
  Pallas kernels: 129 us -> 122 us
    pallas_call x1, Pallas kernels: 126 us -> 119 us  [fused(): pl.pallas_call(functools.partial(fused_kernel, nb, nt, rank, norm_factor)...]
where the time goes in v4:
time: 123 us
  Pallas kernels  122 us (99%)
  between operations  1.29 us (1%)
    pallas_call x1, Pallas kernels, fused(): pl.pallas_call(functools.partial(fused_kernel, nb, nt, rank, norm_factor)...  119 us
    pallas_call x1, Pallas kernels, put_in_place(): pl.pallas_call(functools.partial(place_kernel, rank), out_shape=[jax.Shap...  3.07 us

profile of v4, /device:TPU:1, one launch (start us, length us, event | category | flops | bytes accessed | tf_op | source)
XLA Modules:
  0.0 123.1 jit_solution(6449202637424193390)
XLA Ops:
  1.3 118.7 %fused.1 = (bf16[1,512,1536]{2,1,0:T(8,128)(2,1)}, bf16[160,16,128]{2,1,0:T(8,128)(2,1)}, bf16[64,16,128]{2,1,0:T(8,128)(2,1)}) custom-call(s32[1]{0:T(128)S(6)} %copy.13.step_ref, s32[4,27]{1,0:T(4,128)} %window_ref.1, bf16[1,512,3072]{2,1,0:T(8,128)(2,1)} %hidden_hbm.1, f32[50,2,3072]{2,1,0:T(2,128)} %mod_hbm.1, bf16[96,3072]{1,0:T(8,128)(2,1)} %bitcast.8, ...), custom_call_target="tpu_custom_call" | custom-call | tf_op jit(solution)/shard_map/fused/pallas_call | solution.py:625
  120.0 3.1 %place.1 = (bf16[1,512,1536]{2,1,0:T(8,128)(2,1)}, f32[96,3072]{1,0:T(8,128)}, f32[96,1536]{1,0:T(8,128)}) custom-call(bf16[1,512,1536]{2,1,0:T(8,128)(2,1)} %get-tuple-element.9.att_hbm, bf16[160,16,128]{2,1,0:T(8,128)(2,1)} %get-tuple-element.10.first_hbm, bf16[64,16,128]{2,1,0:T(8,128)(2,1)} %get-tuple-element.11.later_hbm), custom_call_target="tpu_custom_call" | custom-call | tf_op jit(solution)/shard_map/place/pallas_call | solution.py:712

commit v5 on v4

--- a/solution.py
+++ b/solution.py
@@ -81,8 +81,8 @@
 def split_tiles(rank, width, heads, nb, nt):
     one = (rank // ROWS) * (width // LANES)
     ups = (3 * rank // ROWS) * heads
-    spare = min(ups, share_of(one, nb, nt) * nb * nt - one)
-    return 2 * one + ups - spare, one + spare
+    early = (ups - 3 * rank // ROWS) // (nb * nt) * (nb * nt)
+    return early, 2 * one, one + ups - early
 
 
 def sum_shapes(tiles, nb, nt):
@@ -220,10 +220,10 @@
 
 def fused_kernel(nb, nt, rank, norm_factor, step_ref, window_ref, hidden_hbm, mod_hbm, down_hbm, up_hbm,
                  fq_hbm, fk_hbm, fv_hbm, g_hbm,
-                 att_hbm, first_out, later_out,
+                 att_hbm, early_out, first_out, later_out,
                  x_ref, mod_all, mod_ref, down_ref, up_ref, ups, fq_ref, fk_ref, fv_ref, g_ref,
                  swap_ref, relay_ref, low_pack, low_got, low_ref, low_swap, low_relay, bias_ref, q_ref, kl, vl,
-                 probs_s, grad_s, rkv, rq_ref, r_out, r_in, att_ref, up_terms,
+                 probs_f, probs_s, grad_s, rkv, rq_ref, r_out, r_in, att_ref, up_terms,
                  load, att_sem, swap_send, swap_recv, relay_send, relay_recv,
                  low_send, low_recv, r_send, r_recv, *sums):
     place = Place(nb, nt)
@@ -233,10 +233,12 @@
     width = x_ref.shape[1]
     half = rows // 2
     chunks = PARTS * heads
-    per = len(sums) // 2
-    first_tiles, later_tiles = split_tiles(rank, width, heads, nb, nt)
-    first = Sum(place, first_tiles, first_out, sums[:per])
-    later = Sum(place, later_tiles, later_out, sums[per:])
+    per = len(sums) // 3
+    counts = split_tiles(rank, width, heads, nb, nt)
+    outs = (early_out, first_out, later_out)
+    early, first, later = [Sum(place, counts[i], outs[i], sums[i * per:(i + 1) * per])
+                           for i in range(3)]
+    early_tiles = counts[0]
 
     partner = {"tiles": t_index + 1 - 2 * odd}
     target = {"tiles": lax.rem(t_index + 2 - 4 * odd + nt, nt)}
@@ -327,6 +329,7 @@
         for j in range(2):
             r_in[2 * j + 1] = jnp.zeros(r_in.shape[1:], BF16)
 
+    early.clear()
     first.clear()
     later.clear()
     rq_ref[...] = jnp.zeros_like(rq_ref)
@@ -473,7 +476,7 @@
     def pump_next(h, part):
         c = h * PARTS + AHEAD + part
 
-        @pl.when(c < chunks)
+        @pl.when(c < chunks - 2)
         def _():
             pump(c)
 
@@ -483,40 +486,39 @@
             for i in range(2):
                 relay(h * PARTS + 2 * part + i).wait_recv()
 
-    def one_head(h, carry):
-        lanes = pl.ds(pl.multiple_of(h * HEAD, HEAD), HEAD)
+    def own_rows(h, lanes):
         own = dot_nn(low_ref[...], ups[h])
         q_ref[...] = (fq_ref[0, :, lanes].astype(F32) + own[:, 0:HEAD]).astype(BF16)
         kl[0:rows, 0:HEAD] = (fk_ref[0, :, lanes].astype(F32) + own[:, HEAD:2 * HEAD]).astype(BF16)
         vl[0:rows, 0:HEAD] = (fv_ref[0, :, lanes].astype(F32) + own[:, 2 * HEAD:]).astype(BF16)
 
-        arrive(h, 0)
-        arrive(h, 1)
-        for s, (low, got) in enumerate(((low_swap, swap_ref), (low_relay, relay_ref))):
-            add = dot_nn(low[...], ups[h, :, HEAD:])
-            span = slice((s + 1) * rows, (s + 2) * rows)
-            kl[span, 0:HEAD] = (got[h, 0].astype(F32) + add[:, 0:HEAD]).astype(BF16)
-            vl[span, 0:HEAD] = (got[h, 1].astype(F32) + add[:, HEAD:]).astype(BF16)
-        for t in range(rows // TILE):
-            span = slice(t * TILE, (t + 1) * TILE)
-            scores = dot_nt(q_ref[span, :], kl[:, 0:HEAD]) * scale_two + bias_ref[t:t + 1, :]
-            top = jnp.max(scores, axis=1, keepdims=True)
-            weights = jnp.exp2(scores - top)
-            inverse = 1.0 / jnp.sum(weights, axis=1, keepdims=True)
-            probs = weights * inverse
-            prob_grad = dot_nt(g_ref[0, span, lanes], vl[:, 0:HEAD])
-            centre = jnp.sum(probs * prob_grad, axis=1, keepdims=True)
-            probs_s[span, :] = probs.astype(BF16)
-            grad_s[span, :] = (probs * (prob_grad - centre) * scale_root).astype(BF16)
-            if t == 1:
-                pump_next(h, 0)
-        pump_next(h, 1)
+    def softmax(t):
+        span = slice(t * TILE, (t + 1) * TILE)
+        scores = dot_nt(q_ref[span, :], kl[:, 0:HEAD]) * scale_two + bias_ref[t:t + 1, :]
+        top = jnp.max(scores, axis=1, keepdims=True)
+        weights = jnp.exp2(scores - top)
+        inverse = 1.0 / jnp.sum(weights, axis=1, keepdims=True)
+        probs = weights * inverse
+        probs_s[span, :] = probs.astype(BF16)
+        return probs
+
+    def score_grads(t, lanes, probs):
+        span = slice(t * TILE, (t + 1) * TILE)
+        prob_grad = dot_nt(g_ref[0, span, lanes], vl[:, 0:HEAD])
+        centre = jnp.sum(probs * prob_grad, axis=1, keepdims=True)
+        grad_s[span, :] = (probs * (prob_grad - centre) * scale_root).astype(BF16)
+
+    def key_sums(lanes):
+        q_up = dot_nt(up_ref[rank:2 * rank, lanes], q_ref[...]).astype(BF16)
+        rkv[0:rank, :] += dot_nn(q_up, grad_s[...])
+
+    def value_sums(lanes):
+        g_up = dot_nt(up_ref[2 * rank:3 * rank, lanes], g_ref[0, :, lanes]).astype(BF16)
+        rkv[rank:2 * rank, :] += dot_nn(g_up, probs_s[...])
+
+    def outputs(h, lanes):
         q_all = q_ref[...]
         g_all = g_ref[0, :, lanes]
-        q_up = dot_nt(up_ref[rank:2 * rank, lanes], q_all).astype(BF16)
-        g_up = dot_nt(up_ref[2 * rank:3 * rank, lanes], g_all).astype(BF16)
-        rkv[0:rank, :] += dot_nn(q_up, grad_s[...])
-        rkv[rank:2 * rank, :] += dot_nn(g_up, probs_s[...])
         att = dot_nn(probs_s[...], vl[...])
         att_ref[h] = att[:, 0:HEAD].astype(BF16)
         att_copy(h).start()
@@ -531,13 +533,60 @@
                 start = j * rank + r * ROWS
                 spot = h * (3 * rank // ROWS) + start // ROWS
                 up_terms[spot] = (term[start:start + ROWS] * norm_factor).astype(BF16)
-        pump_next(h, 2)
-        pump_next(h, 3)
+
+    def one_head(h, carry):
+        lanes = pl.ds(pl.multiple_of(h * HEAD, HEAD), HEAD)
+        own_rows(h, lanes)
+        arrive(h, 0)
+        arrive(h, 1)
+        for s, (low, got) in enumerate(((low_swap, swap_ref), (low_relay, relay_ref))):
+            add = dot_nn(low[...], ups[h, :, HEAD:])
+            span = slice((s + 1) * rows, (s + 2) * rows)
+            kl[span, 0:HEAD] = (got[h, 0].astype(F32) + add[:, 0:HEAD]).astype(BF16)
+            vl[span, 0:HEAD] = (got[h, 1].astype(F32) + add[:, HEAD:]).astype(BF16)
+        for t in range(rows // TILE):
+            score_grads(t, lanes, softmax(t))
+            if t == 1:
+                pump(jnp.minimum(h * PARTS + AHEAD, chunks - 2))
+        pump(jnp.minimum(h * PARTS + AHEAD + 1, chunks - 1))
+        key_sums(lanes)
+        value_sums(lanes)
+        outputs(h, lanes)
+        for part in (2, 3):
+            pump_next(h, part)
         return carry
 
-    lax.fori_loop(0, heads, one_head, 0)
+    lax.fori_loop(0, heads - 1, one_head, 0)
+    if early_tiles:
+        early.terms[0:early_tiles] = up_terms[0:early_tiles]
+        early.pair_start()
+    else:
+        early_out[...] = jnp.zeros_like(early_out)
+    last = heads - 1
+    lanes = slice(last * HEAD, heads * HEAD)
+    own_rows(last, lanes)
+
+    def rebuild(dst, part):
+        for s, (low, got) in enumerate(((low_swap, swap_ref), (low_relay, relay_ref))):
+            add = dot_nn(low[...], ups[last, :, (part + 1) * HEAD:(part + 2) * HEAD])
+            dst[(s + 1) * rows:(s + 2) * rows, 0:HEAD] = (
+                got[last, part].astype(F32) + add).astype(BF16)
+
+    arrive(last, 0)
+    rebuild(kl, 0)
+    for t in range(rows // TILE):
+        probs_f[t * TILE:(t + 1) * TILE, :] = softmax(t)
+    value_sums(lanes)
     send_back(value_return, rank)
+    arrive(last, 1)
+    rebuild(vl, 1)
+    for t in range(rows // TILE):
+        score_grads(t, lanes, probs_f[t * TILE:(t + 1) * TILE, :])
+    key_sums(lanes)
     send_back(key_return, 0)
+    if early_tiles:
+        early.xy_start()
+    outputs(last, lanes)
 
     def down_dot(total, grads, count):
         def columns(i, carry):
@@ -552,27 +601,33 @@
         lax.fori_loop(0, width // (2 * LANES), columns, 0)
 
     one = (rank // ROWS) * (width // LANES)
-    kept = first_tiles - 2 * one
-    if kept:
-        first.terms[2 * one:first_tiles] = up_terms[0:kept]
-    if later_tiles > one:
-        later.terms[one:later_tiles] = up_terms[kept:]
+    later.terms[one:counts[2]] = up_terms[early_tiles:]
     grads = jnp.concatenate([rq_ref[...].astype(BF16), take_back(value_return, rank)], axis=0)
     down_dot(first, grads, 2 * rank // ROWS)
     first.pair_start()
+    if early_tiles:
+        early.z_start()
     grads = take_back(key_return, 0)
     down_dot(later, grads, rank // ROWS)
     later.pair_start()
     first.xy_start()
+    if early_tiles:
+        early.z_back()
     later.xy_start()
     first.z_start()
+    if early_tiles:
+        early.xy_back()
     later.z_start()
     first.z_back()
+    if early_tiles:
+        early.pair_back()
     later.z_back()
     first.xy_back()
     later.xy_back()
     first.pair_back()
     later.pair_back()
+    if early_tiles:
+        early.finish()
     first.finish()
     later.finish()
 
@@ -604,6 +659,7 @@
             ready(1).wait_send()
 
     lax.fori_loop(0, heads, lambda h, carry: (att_copy(h).wait(), carry)[1], 0)
+    early.drain()
     first.drain()
     later.drain()
 
@@ -620,17 +676,15 @@
     whole = pl.BlockSpec(memory_space=pltpu.VMEM)
     chunks = PARTS * heads
     blocks = rows // TILE
-    first_tiles, later_tiles = split_tiles(rank, width, heads, nb, nt)
-    totals = [share_of(tiles, nb, nt) * nb * nt for tiles in (first_tiles, later_tiles)]
+    counts = [max(tiles, 1) for tiles in split_tiles(rank, width, heads, nb, nt)]
+    totals = [share_of(tiles, nb, nt) * nb * nt for tiles in counts]
     return pl.pallas_call(
         functools.partial(fused_kernel, nb, nt, rank, norm_factor),
         out_shape=[
             jax.ShapeDtypeStruct((1, rows, across), BF16),
-            jax.ShapeDtypeStruct((totals[0], ROWS, LANES), BF16),
-            jax.ShapeDtypeStruct((totals[1], ROWS, LANES), BF16),
-        ],
+        ] + [jax.ShapeDtypeStruct((total, ROWS, LANES), BF16) for total in totals],
         in_specs=[smem, smem] + [anywhere] * 8,
-        out_specs=[anywhere, whole, whole],
+        out_specs=[anywhere, whole, whole, whole],
         scratch_shapes=[
             vmem((rows, width), BF16), vmem(modulation.shape, F32), vmem((2, width), F32),
             vmem((LANES, width), BF16), vmem(up.shape, BF16), vmem((heads, LANES, 3 * HEAD), BF16),
@@ -640,6 +694,7 @@
             vmem((rows, LANES), BF16), vmem((rows, LANES), BF16), vmem((rows, LANES), BF16),
             vmem((8, 3 * rows), F32), vmem((rows, HEAD), BF16),
             vmem((3 * rows, 2 * HEAD), BF16), vmem((3 * rows, 2 * HEAD), BF16),
+            vmem((rows, 3 * rows), F32),
             vmem((rows, 3 * rows), BF16), vmem((rows, 3 * rows), BF16),
             vmem((2 * rank, 3 * rows), F32), vmem((rank, rows), F32),
             vmem((4, rank, rows), BF16), vmem((4, rank, rows), BF16),
@@ -647,7 +702,7 @@
             dma((blocks + 7,)), dma((heads,)),
             dma((chunks,)), dma((chunks,)), dma((chunks,)), dma((chunks,)),
             dma((4,)), dma((4,)), dma((4,)), dma((4,)),
-        ] + sum_shapes(first_tiles, nb, nt) + sum_shapes(later_tiles, nb, nt),
+        ] + sum([sum_shapes(tiles, nb, nt) for tiles in counts], []),
         compiler_params=pltpu.CompilerParams(
             collective_id=0, has_side_effects=True, vmem_limit_bytes=60 << 20
         ),
@@ -655,8 +710,8 @@
     )(step, window, hidden, modulation, down, up, fq, fk, fv, g)
 
 
-def place_kernel(rank, att_hbm, first_hbm, later_hbm, att_out, down_out, up_out,
-                 att_ref, first_ref, later_ref, down_ref, up_ref, load, store):
+def place_kernel(rank, early_tiles, att_hbm, early_hbm, first_hbm, later_hbm,
+                 att_out, down_out, up_out, att_ref, early_ref, first_ref, later_ref, down_ref, up_ref, load, store):
     rows, across = att_ref.shape[1:]
     heads = across // HEAD
     width = down_ref.shape[1]
@@ -664,7 +719,8 @@
     parts = 4
     cut = rows // parts
     takes = [pltpu.make_async_copy(first_hbm, first_ref, load.at[0]),
-             pltpu.make_async_copy(later_hbm, later_ref, load.at[1])]
+             pltpu.make_async_copy(later_hbm, later_ref, load.at[1]),
+             pltpu.make_async_copy(early_hbm, early_ref, load.at[6])]
     moves = [(pltpu.make_async_copy(att_hbm.at[:, pl.ds(i * cut, cut)],
                                     att_ref.at[:, pl.ds(i * cut, cut)], load.at[2 + i]),
               pltpu.make_async_copy(att_ref.at[:, pl.ds(i * cut, cut)],
@@ -686,13 +742,11 @@
                 down_ref[j * rank + r * ROWS:j * rank + (r + 1) * ROWS, lanes] = tile.astype(F32)
     down_store = pltpu.make_async_copy(down_ref, down_out, store.at[0])
     down_store.start()
-    spare = min(3 * step * heads, later_ref.shape[0] - one)
-    kept = 3 * step * heads - spare
     for h in range(heads):
         lanes = slice(h * HEAD, (h + 1) * HEAD)
         for r in range(3 * step):
             k = h * 3 * step + r
-            tile = first_ref[2 * one + k] if k < kept else later_ref[one + k - kept]
+            tile = early_ref[k] if k < early_tiles else later_ref[one + k - early_tiles]
             up_ref[r * ROWS:(r + 1) * ROWS, lanes] = tile.astype(F32)
     up_store = pltpu.make_async_copy(up_ref, up_out, store.at[1])
     up_store.start()
@@ -705,25 +759,25 @@
     up_store.wait()
 
 
-def put_in_place(rank, width, attended, first, later):
+def put_in_place(rank, width, early_tiles, attended, early, first, later):
     across = attended.shape[2]
     vmem, dma = pltpu.VMEM, pltpu.SemaphoreType.DMA
     anywhere = pl.BlockSpec(memory_space=pl.ANY)
     return pl.pallas_call(
-        functools.partial(place_kernel, rank),
+        functools.partial(place_kernel, rank, early_tiles),
         out_shape=[
             jax.ShapeDtypeStruct(attended.shape, BF16),
             jax.ShapeDtypeStruct((3 * rank, width), F32),
             jax.ShapeDtypeStruct((3 * rank, across), F32),
         ],
-        in_specs=[anywhere] * 3,
+        in_specs=[anywhere] * 4,
         out_specs=[anywhere] * 3,
         scratch_shapes=[
-            vmem(attended.shape, BF16), vmem(first.shape, BF16), vmem(later.shape, BF16),
-            vmem((3 * rank, width), F32), vmem((3 * rank, across), F32), dma((6,)), dma((6,)),
+            vmem(attended.shape, BF16), vmem(early.shape, BF16), vmem(first.shape, BF16), vmem(later.shape, BF16),
+            vmem((3 * rank, width), F32), vmem((3 * rank, across), F32), dma((7,)), dma((6,)),
         ],
         name="place",
-    )(attended, first, later)
+    )(attended, early, first, later)
 
 
 def per_device(
@@ -745,11 +799,15 @@
     norm_factor = 1.0 / math.sqrt(hidden.shape[0] * nb * slab_rows * nt)
     down = adapter_down_weight.transpose(0, 2, 1).reshape(3 * rank, width)
     up = adapter_up_weight.reshape(3 * rank, across)
-    attended, first, later = fused(
+    heads = across // HEAD
+    early_tiles = split_tiles(rank, width, heads, nb, nt)[0]
+    attended, early, first, later = fused(
         nb, nt, norm_factor, truncation_step, window, hidden, modulation, down, up,
         frozen_queries, frozen_keys, frozen_values, reward_output_gradient,
     )
-    attended, grad_down, grad_up = put_in_place(rank, width, attended, first, later)
+    attended, grad_down, grad_up = put_in_place(
+        rank, width, early_tiles, attended, early, first, later
+    )
     grad_down = grad_down.reshape(3, rank, width).transpose(0, 2, 1)
     grad_up = grad_up.reshape(3, rank, across)
     return (attended, grad_down, grad_up)

time: 123 us -> 120 us (0.976)
  Pallas kernels: 122 us -> 118 us
    pallas_call x1, Pallas kernels: 119 us -> 115 us  [fused(): pl.pallas_call(functools.partial(fused_kernel, nb, nt, rank, norm_factor)...]
where the time goes in v5:
time: 120 us
  Pallas kernels  118 us (98%)
  between operations  1.29 us (1%)
    pallas_call x1, Pallas kernels, fused(): pl.pallas_call(functools.partial(fused_kernel, nb, nt, rank, norm_factor)...  115 us
    pallas_call x1, Pallas kernels, put_in_place(): pl.pallas_call(functools.partial(place_kernel, rank, early_tiles), out_sh...  3.08 us

profile of v5, /device:TPU:1, one launch (start us, length us, event | category | flops | bytes accessed | tf_op | source)
XLA Modules:
  0.0 119.7 jit_solution(10692511144624904587)
XLA Ops:
  1.3 115.3 %fused.1 = (bf16[1,512,1536]{2,1,0:T(8,128)(2,1)}, bf16[64,16,128]{2,1,0:T(8,128)(2,1)}, bf16[96,16,128]{2,1,0:T(8,128)(2,1)}, bf16[64,16,128]{2,1,0:T(8,128)(2,1)}) custom-call(s32[1]{0:T(128)S(6)} %copy.13.step_ref, s32[4,27]{1,0:T(4,128)} %window_ref.1, bf16[1,512,3072]{2,1,0:T(8,128)(2,1)} %hidden_hbm.1, f32[50,2,3072]{2,1,0:T(2,128)} %mod_hbm.1, ...), custom_call_target="tpu_custom_call" | custom-call | tf_op jit(solution)/shard_map/fused/pallas_call | solution.py:681
  116.6 3.1 %place.1 = (bf16[1,512,1536]{2,1,0:T(8,128)(2,1)}, f32[96,3072]{1,0:T(8,128)}, f32[96,1536]{1,0:T(8,128)}) custom-call(bf16[1,512,1536]{2,1,0:T(8,128)(2,1)} %get-tuple-element.10.att_hbm, bf16[64,16,128]{2,1,0:T(8,128)(2,1)} %get-tuple-element.11.early_hbm, bf16[96,16,128]{2,1,0:T(8,128)(2,1)} %get-tuple-element.12.first_hbm, ...), custom_call_target="tpu_custom_call" | custom-call | tf_op jit(solution)/shard_map/place/pallas_call | solution.py:766

commit v6 on v5

--- a/solution.py
+++ b/solution.py
@@ -611,17 +611,17 @@
     down_dot(later, grads, rank // ROWS)
     later.pair_start()
     first.xy_start()
+    later.xy_start()
     if early_tiles:
         early.z_back()
-    later.xy_start()
     first.z_start()
+    later.z_start()
     if early_tiles:
         early.xy_back()
-    later.z_start()
     first.z_back()
+    later.z_back()
     if early_tiles:
         early.pair_back()
-    later.z_back()
     first.xy_back()
     later.xy_back()
     first.pair_back()

time: 120 us -> 120 us (level)
  no operation moved by 1% of the time
where the time goes in v6:
time: 120 us
  Pallas kernels  118 us (98%)
  between operations  1.29 us (1%)
    pallas_call x1, Pallas kernels, fused(): pl.pallas_call(functools.partial(fused_kernel, nb, nt, rank, norm_factor)...  115 us
    pallas_call x1, Pallas kernels, put_in_place(): pl.pallas_call(functools.partial(place_kernel, rank, early_tiles), out_sh...  3.08 us

profile of v6, /device:TPU:1, one launch (start us, length us, event | category | flops | bytes accessed | tf_op | source)
XLA Modules:
  0.0 119.6 jit_solution(16697597963711349284)
XLA Ops:
  1.3 115.2 %fused.1 = (bf16[1,512,1536]{2,1,0:T(8,128)(2,1)}, bf16[64,16,128]{2,1,0:T(8,128)(2,1)}, bf16[96,16,128]{2,1,0:T(8,128)(2,1)}, bf16[64,16,128]{2,1,0:T(8,128)(2,1)}) custom-call(s32[1]{0:T(128)S(6)} %copy.13.step_ref, s32[4,27]{1,0:T(4,128)} %window_ref.1, bf16[1,512,3072]{2,1,0:T(8,128)(2,1)} %hidden_hbm.1, f32[50,2,3072]{2,1,0:T(2,128)} %mod_hbm.1, ...), custom_call_target="tpu_custom_call" | custom-call | tf_op jit(solution)/shard_map/fused/pallas_call | solution.py:681
  116.5 3.1 %place.1 = (bf16[1,512,1536]{2,1,0:T(8,128)(2,1)}, f32[96,3072]{1,0:T(8,128)}, f32[96,1536]{1,0:T(8,128)}) custom-call(bf16[1,512,1536]{2,1,0:T(8,128)(2,1)} %get-tuple-element.10.att_hbm, bf16[64,16,128]{2,1,0:T(8,128)(2,1)} %get-tuple-element.11.early_hbm, bf16[96,16,128]{2,1,0:T(8,128)(2,1)} %get-tuple-element.12.first_hbm, ...), custom_call_target="tpu_custom_call" | custom-call | tf_op jit(solution)/shard_map/place/pallas_call | solution.py:766
